TPU v7x, 512 devices: a whole 4x8x8 slice. The times are simulated.
512 devices in a mesh: row: 32 (over y, x), head: 16 (over z, core).
Axes of the slice: x: 4, y: 8, z: 8, core: 2. Of those that a mesh axis runs over, the one named last changes fastest.
Arguments:
- patches: bfloat16 [196608, 768], P(('row', 'head')), may hold values from -6 to 6
- w_patch: bfloat16 [768, 1024], replicated, may hold values from -0.21875 to 0.21875
- patch_bias: float32 [1024], replicated, may hold values from -4 to 4
- w_kv: bfloat16 [1024, 2048], P(None, 'head'), may hold values from -0.1875 to 0.1875
- queries: bfloat16 [2048, 1024], P(None, 'head'), may hold values from -160 to 160
Outputs:
- readout: bfloat16 [2048, 1024], P(None, 'head')
All inputs are finite; a program needn't handle non-finite values.
Results may differ from a plain program's by a relative error of at most 0.011.
Values may be sent and summed in bfloat16 or wider, within the bound.
No kernel may reach another device: no remote copies, remote signals or barrier semaphores. Data moves between devices by JAX's collectives and lax.ppermute only.
A program may use at most 128 MiB of HBM per device.

v0:
```python
import jax
import jax.numpy as jnp
from jax import lax
from jax.sharding import PartitionSpec as P


def body(patches, w_patch, patch_bias, w_kv, queries):
    embed = jnp.dot(patches, w_patch, preferred_element_type=jnp.float32) + patch_bias
    mean = jnp.mean(embed, axis=-1, keepdims=True)
    var = jnp.mean((embed - mean) * (embed - mean), axis=-1, keepdims=True)
    normed = ((embed - mean) * lax.rsqrt(var + 1e-05)).astype(jnp.bfloat16)
    head_size = queries.shape[1]
    latents = queries.shape[0]
    kv_all = jnp.dot(
        normed, lax.all_gather(w_kv, "head", axis=1, tiled=True), preferred_element_type=jnp.float32
    ).astype(jnp.bfloat16)
    kv = lax.all_to_all(kv_all, "head", split_axis=1, concat_axis=0, tiled=True)
    rows = kv.shape[0]
    block = min(512, rows)
    blocks = kv.reshape(rows // block, block, 2 * head_size)
    scale = float(head_size) ** (-0.5)

    def step(carry, piece):
        run_max, total, accum = carry
        scores = (
            jnp.dot(queries, piece[:, :head_size].T, preferred_element_type=jnp.float32) * scale
        )
        new_max = jnp.maximum(run_max, jnp.max(scores, axis=1))
        factor = jnp.exp(run_max - new_max)
        probs = jnp.exp(scores - new_max[:, None])
        total = total * factor + jnp.sum(probs, axis=1)
        accum = accum * factor[:, None] + jnp.dot(
            probs.astype(jnp.bfloat16), piece[:, head_size:], preferred_element_type=jnp.float32
        )
        return ((new_max, total, accum), None)

    start = (
        jnp.full((latents,), -jnp.inf, jnp.float32),
        jnp.zeros((latents,), jnp.float32),
        jnp.zeros((latents, head_size), jnp.float32),
    )
    (run_max, total, accum), _ = lax.scan(step, start, blocks)
    top = lax.pmax(run_max, "row")
    factor = jnp.exp(run_max - top)
    whole, summed = lax.psum((total * factor, accum * factor[:, None]), "row")
    return (summed / whole[:, None]).astype(jnp.bfloat16)


def solution(mesh):
    placed = (P(("row", "head"), None), P(), P(), P(None, "head"), P(None, "head"))
    return jax.shard_map(
        body, mesh=mesh, in_specs=placed, out_specs=P(None, "head"), check_vma=False
    )
```

profile of v0, /device:TPU:64, one launch (start us, length us, event | category | flops | bytes accessed | tf_op | source)
XLA Modules:
  0.0 447.2 jit_solution(7872800311003511222)
XLA Ops:
  6.5 0.7 all-gather.2.cloned.1.call-update
  7.3 0.7 copy-done
  7.9 1.9 fusion.14
  10.2 55.2 %all-gather.2.cloned.1.call-done = bf16[1024,2048]{1,0:T(8,128)(2,1)} async-done(((bf16[1024,128]{1,0:T(8,128)(2,1)}), bf16[1024,2048]{1,0:T(8,128)(2,1)}) %all-gather.2.cloned.1.call-update) | async-done | bytes 4194320 | tf_op jit(solution)/shard_map/all_gather | solution.py:15
  65.4 4.1 fusion.10
  69.5 1.6 copy.10
  71.1 5.3 %all-to-all-start = ((bf16[384,16,128]{2,0,1:T(8,128)(2,1)}), bf16[384,16,128]{2,0,1:T(8,128)(2,1)}, u32[]{:S(2)}, u32[]{:S(2)}) async-start(bf16[384,16,128]{2,0,1:T(8,128)(2,1)} %bitcast.18), calls=%async_computation | async-start | bytes 3145728 | tf_op jit(solution)/shard_map/all_to_all | solution.py:17
  76.5 36.1 %all-to-all-done = bf16[384,16,128]{2,0,1:T(8,128)(2,1)} async-done(((bf16[384,16,128]{2,0,1:T(8,128)(2,1)}), bf16[384,16,128]{2,0,1:T(8,128)(2,1)}, u32[]{:S(2)}, u32[]{:S(2)}) %all-to-all-start) | async-done | bytes 1572896 | tf_op jit(solution)/shard_map/all_to_all | solution.py:17
  112.5 95.5 %while.15 = (s32[]{:T(128)}, f32[2048]{0:T(1024)S(1)}, f32[2048]{0:T(1024)S(1)}, f32[2048,64]{0,1:T(8,128)S(1)}, bf16[12,512,128]{2,1,0:T(8,128)(2,1)}, /*index=5*/bf16[2048,64]{0,1:T(8,128)(2,1)S(1)}, s32[]{:T(128)}, s32[]{:T(128)}) while((s32[]{:T(128)}, f32[2048]{0:T(1024)S(1)}, f32[2048]{0:T(1024)S(1)}, ...), condition=%wide.region_5.6_spmd.clone, body=%wide.region_2.5_spmd.clone.sunk | while | flops 277227520 | bytes 31326336 | solution.py:42
  112.5 0.9 dynamic-slice_bitcast_fusion.2
  113.5 2.6 multiply_reduce_fusion.3
  116.1 3.0 fusion.27
  119.5 0.9 convolution_add_fusion.3
  120.5 0.9 dynamic-slice_bitcast_fusion.2
  121.4 2.6 multiply_reduce_fusion.3
  124.0 3.0 fusion.27
  127.5 0.9 convolution_add_fusion.3
  128.5 0.9 dynamic-slice_bitcast_fusion.2
  129.4 2.6 multiply_reduce_fusion.3
  132.0 3.0 fusion.27
  135.1 0.4 copy-done.1
  135.5 0.9 convolution_add_fusion.3
  136.4 0.9 dynamic-slice_bitcast_fusion.2
  137.4 2.6 multiply_reduce_fusion.3
  140.0 3.0 fusion.27
  143.4 0.9 convolution_add_fusion.3
  144.4 0.9 dynamic-slice_bitcast_fusion.2
  145.3 2.6 multiply_reduce_fusion.3
  147.9 3.0 fusion.27
  151.0 0.4 copy-done.1
  151.4 0.9 convolution_add_fusion.3
  152.3 0.9 dynamic-slice_bitcast_fusion.2
  153.3 2.6 multiply_reduce_fusion.3
  155.9 3.0 fusion.27
  159.3 0.9 convolution_add_fusion.3
  160.3 0.9 dynamic-slice_bitcast_fusion.2
  161.2 2.6 multiply_reduce_fusion.3
  163.8 3.0 fusion.27
  167.3 0.9 convolution_add_fusion.3
  168.3 0.9 dynamic-slice_bitcast_fusion.2
  169.2 2.6 multiply_reduce_fusion.3
  171.8 3.0 fusion.27
  175.2 0.9 convolution_add_fusion.3
  176.2 0.9 dynamic-slice_bitcast_fusion.2
  177.1 2.6 multiply_reduce_fusion.3
  179.8 3.0 fusion.27
  183.2 0.9 convolution_add_fusion.3
  184.2 0.9 dynamic-slice_bitcast_fusion.2
  185.1 2.6 multiply_reduce_fusion.3
  187.7 3.0 fusion.27
  191.2 0.9 convolution_add_fusion.3
  192.1 0.9 dynamic-slice_bitcast_fusion.2
  193.1 2.6 multiply_reduce_fusion.3
  195.7 3.0 fusion.27
  199.1 0.9 convolution_add_fusion.3
  200.1 0.9 dynamic-slice_bitcast_fusion.2
  201.0 2.6 multiply_reduce_fusion.3
  203.6 3.0 fusion.27
  207.1 0.9 convolution_add_fusion.3
  208.0 75.6 %pmax.7 = f32[2048]{0:T(1024)S(1)} all-reduce(f32[2048]{0:T(1024)S(1)} %get-tuple-element.40), channel_id=1, replica_groups=mesh['row'=32,'head'=16] {'row'}, use_global_device_ids=true, to_apply=%region_6.7 | all-reduce | flops 2048 | bytes 16384 | tf_op jit(solution)/shard_map/pmax | solution.py:43
  283.7 0.9 broadcast_multiply_fusion
  284.6 70.7 %psum.15 = f32[2048]{0:T(1024)S(1)} all-reduce(f32[2048]{0:T(1024)S(1)} %get-tuple-element.77), channel_id=1, replica_groups=mesh['row'=32,'head'=16] {'row'}, use_global_device_ids=true, to_apply=%region_8.9 | all-reduce | flops 2048 | bytes 16384 | tf_op jit(solution)/shard_map/psum | solution.py:45
  355.3 83.3 %all-reduce.2.cloned.1.call-done = f32[2048,64]{0,1:T(8,128)} async-done(((f32[2048,64]{0,1:T(8,128)}), f32[2048,64]{0,1:T(8,128)}) %all-reduce.2.cloned.1.call-update) | async-done | bytes 524304 | tf_op jit(solution)/shard_map/psum | solution.py:45
  438.6 1.8 divide_convert_fusion
  (71 shorter events, 4.5 us)
Async XLA Ops:
  6.5 1.4 copy-start
  6.5 58.9 %all-gather.2.cloned.1.call-start = ((), (), s32[]{:S(2)}) async-start(), calls=%async_computation.1 | async-start | bytes 4456448 | tf_op jit(solution)/shard_map/all_gather | solution.py:15
  71.1 41.5 %copy-start.2 = (bf16[2048,64]{0,1:T(8,128)(2,1)S(1)}, bf16[2048,64]{0,1:T(8,128)(2,1)}, u32[]{:S(2)}) copy-start(bf16[2048,64]{0,1:T(8,128)(2,1)} %param.11) | copy-start | bytes 786436
  71.1 41.5 %all-to-all-start = ((bf16[384,16,128]{2,0,1:T(8,128)(2,1)}), bf16[384,16,128]{2,0,1:T(8,128)(2,1)}, u32[]{:S(2)}, u32[]{:S(2)}) async-start(bf16[384,16,128]{2,0,1:T(8,128)(2,1)} %bitcast.18), calls=%async_computation | async-start | bytes 3145728 | tf_op jit(solution)/shard_map/all_to_all | solution.py:17
  76.4 362.2 %all-reduce.2.cloned.1.call-start = ((), (), s32[]{:S(2)}) async-start(), calls=%async_computation.2 | async-start | bytes 1048576 | tf_op jit(solution)/shard_map/psum | solution.py:45
  116.1 3.4 copy-start.1
  124.0 3.4 copy-start.1
  132.0 3.4 copy-start.1
  140.0 3.4 copy-start.1
  147.9 3.4 copy-start.1
  155.9 3.4 copy-start.1
  163.8 3.4 copy-start.1
  171.8 3.4 copy-start.1
  179.8 3.4 copy-start.1
  187.7 3.4 copy-start.1
  195.7 3.4 copy-start.1
  203.6 3.4 copy-start.1
Sparse Core Ops, SparseCore 0:
  9.4 55.9 all-gather.1
  284.7 153.8 all-reduce.1
where the time goes:
time: 448 us; the launch traced here: 447 us
  waiting for transfers between devices  175 us (39%)
  blocking collectives  146 us (33%)
  matrix products  48.6 us (11%)
  other arithmetic  39.7 us (9%)
  local copies, waits for them, and re-layouts  17.9 us (4%)
  between operations  13.5 us (3%)
  starting transfers between devices  5.38 us (1%)
    psum x1, waiting for transfers between devices, body(): whole, summed = lax.psum((total * factor, accum * factor[:, None]), 'row')  83.3 us
    pmax x1, blocking collectives, body(): top = lax.pmax(run_max, 'row')  75.6 us
    psum x1, blocking collectives, body(): whole, summed = lax.psum((total * factor, accum * factor[:, None]), 'row')  70.7 us
    all_gather x1, waiting for transfers between devices, body(): lax.all_gather(w_kv, 'head', axis=1, tiled=True)  55.2 us
    reduce_sum x12, other arithmetic, step(): total = total * factor + jnp.sum(probs, axis=1)  36.6 us
    all_to_all x1, waiting for transfers between devices, body(): kv = lax.all_to_all(kv_all, 'head', split_axis=1, concat_axis=0, tiled=True)  36.1 us
    dot_general x12, matrix products, step(): jnp.dot(queries, piece[:, :head_size].T, preferred_element_type=jnp.float32)  31.3 us
    dot_general x12, matrix products, step(): jnp.dot(probs.astype(jnp.bfloat16), piece[:, head_size:], preferred_eleme...  11.3 us
  transfers between devices with their start and end apart: 3, of which 3 were waited for; matrix products, arithmetic and copies ran while one was open for 1% of the time, Pallas kernels for 0%

commit v1 on v0

v1 whole, which is shorter than its diff:
```python
import functools

import jax
import jax.numpy as jnp
from jax import lax
from jax.experimental import pallas as pl
from jax.experimental.pallas import tpu as pltpu
from jax.sharding import Mesh
from jax.sharding import PartitionSpec as P

F32 = jnp.float32
BF16 = jnp.bfloat16
LOG2E = 1.4426950408889634
LIMIT = 2.0**64
CHUNKS = 1
BLOCK = 1024
ROWS = 80
PAY = 48
PLAIN = (((1,), (0,)), ((), ()))


def split(value):
    high = value.astype(BF16)
    return high, (value - high.astype(F32)).astype(BF16)


def attend_kernel(first, last, block, *refs):
    if first:
        x_ref, rstd_ref, w_ref, b_ref, q_ref = refs[:5]
        rest = refs[5:]
    else:
        x_ref, rstd_ref, w_ref, b_ref, q_ref, acc_in, m_in = refs[:7]
        rest = refs[7:]
    if last:
        pay_ref, k_ref, v_ref, qa_ref, m_ref, acc_ref = rest
    else:
        acc_ref, m_ref, k_ref, v_ref, qa_ref = rest
    tokens = x_ref.shape[0]
    heads, size, latents = q_ref.shape
    steps = tokens // block

    def at(t):
        return pl.ds(pl.multiple_of(t * block, block), block)

    def project(t, carry):
        kv = jnp.dot(x_ref[at(t), :], w_ref[...], preferred_element_type=F32)
        kv = (kv + b_ref[...]) * rstd_ref[at(t), :]
        lane = lax.broadcasted_iota(jnp.int32, (block, 2 * size), 1)
        for h in range(heads):
            mine = kv[:, 2 * size * h : 2 * size * (h + 1)]
            k_ref[h, at(t), :] = jnp.where(lane < size, mine, 1.0).astype(BF16)
            v_ref[h, t, :size, :] = mine.T[size:, :].astype(BF16)
            v_ref[h, t, size:, :] = jnp.ones((ROWS - size, block), BF16)
        return carry

    lax.fori_loop(0, steps, project, 0, unroll=2)

    def scores(h, keys):
        return lax.dot_general(k_ref[h, keys, :], qa_ref[h], PLAIN, preferred_element_type=F32)

    def set_max(h, value):
        high, low = split(value)
        m_ref[h] = high.astype(F32) + low.astype(F32)
        qa_ref[h, size : size + 16, :] = jnp.concatenate(
            [-high, -low, jnp.zeros((14, latents), BF16)], axis=0
        )

    for h in range(heads):
        qa_ref[h, :size, :] = q_ref[h]
        qa_ref[h, size:, :] = jnp.zeros((size, latents), BF16)
        if first:
            set_max(h, jnp.max(scores(h, pl.ds(0, 128)), axis=0, keepdims=True))
        else:
            set_max(h, m_in[h])

    def sweep(h):
        for t in range(steps):
            probs = jnp.exp2(scores(h, pl.ds(t * block, block))).astype(BF16)
            acc_ref[h] += lax.dot_general(v_ref[h, t], probs, PLAIN, preferred_element_type=F32)

    for h in range(heads):
        acc_ref[h] = jnp.zeros((ROWS, latents), F32) if first else acc_in[h]
        sweep(h)

        @pl.when(jnp.logical_not(jnp.max(acc_ref[h, size : size + 8, :]) < LIMIT))
        def _(h=h):
            before = m_ref[h]
            qa_ref[h, size:, :] = jnp.zeros((size, latents), BF16)

            def widen(t, best):
                return jnp.maximum(best, jnp.max(scores(h, at(t)), axis=0, keepdims=True))

            set_max(h, lax.fori_loop(0, steps, widen, before))
            if first:
                acc_ref[h] = jnp.zeros((ROWS, latents), F32)
            else:
                acc_ref[h] = acc_in[h] * jnp.exp2(before - m_ref[h])

            def redo(t, carry):
                probs = jnp.exp2(scores(h, at(t))).astype(BF16)
                acc_ref[h] += lax.dot_general(v_ref[h, t], probs, PLAIN, preferred_element_type=F32)
                return carry

            lax.fori_loop(0, steps, redo, 0)

        if last:
            for i in range(latents // 128):
                lanes = pl.ds(128 * i, 128)
                acc, total, m = acc_ref[h, :size, lanes], acc_ref[h, size : size + 1, lanes], m_ref[h, :, lanes]
                for side in range(2):
                    pay_ref[h, 2 * i + side] = pack(fold_half(acc, side), both(total, side), both(m, side))


def both(row, side):
    lane = lax.broadcasted_iota(jnp.int32, row.shape, 1)
    keep = lane < 64 if side == 0 else lane >= 64
    return jnp.where(keep, row, pltpu.roll(row, 64, 1))


def fold_half(acc, side):
    half = acc.shape[0] // 2
    low, high = acc[:half], acc[half:]
    if side == 0:
        high = pltpu.roll(high, 64, 1)
    else:
        low = pltpu.roll(low, 64, 1)
    lane = lax.broadcasted_iota(jnp.int32, low.shape, 1)
    return jnp.where(lane < 64, low, high)


def pack(acc, total, m):
    t_high, m_high = total.astype(BF16).astype(F32), m.astype(BF16).astype(F32)
    fill = jnp.zeros((PAY - acc.shape[0] - 4, acc.shape[1]), F32)
    rows = [acc, t_high, total - t_high, m_high, m - m_high, fill]
    return jnp.concatenate(rows, axis=0).astype(BF16)


def attend(x, rstd, w, b, q, state, last):
    tokens = x.shape[0]
    heads, size, latents = q.shape
    block = min(BLOCK, tokens)
    first = state is None
    vmem = pl.BlockSpec(memory_space=pltpu.VMEM)
    acc = jax.ShapeDtypeStruct((heads, ROWS, latents), F32)
    m = jax.ShapeDtypeStruct((heads, 1, latents), F32)
    scratch = [
        pltpu.VMEM((heads, tokens, 2 * size), BF16),
        pltpu.VMEM((heads, tokens // block, ROWS, block), BF16),
        pltpu.VMEM((heads, 2 * size, latents), BF16),
    ]
    if last:
        out = jax.ShapeDtypeStruct((heads, latents // 64, PAY, 128), BF16)
        scratch += [pltpu.VMEM(m.shape, F32), pltpu.VMEM(acc.shape, F32)]
    else:
        out = (acc, m)
    ins = (x, rstd, w, b, q) + (() if first else tuple(state))
    work = tokens * latents * heads
    return pl.pallas_call(
        functools.partial(attend_kernel, first, last, block),
        out_shape=out,
        in_specs=[vmem] * len(ins),
        out_specs=jax.tree.map(lambda _: vmem, out),
        scratch_shapes=scratch,
        compiler_params=pltpu.CompilerParams(vmem_limit_bytes=56 << 20),
        cost_estimate=pl.CostEstimate(
            flops=16 * work * size, bytes_accessed=x.size * 2, transcendentals=work
        ),
        name="attend",
    )(*ins)


def combine_kernel(final, parts_ref, out_ref):
    count, blocks = parts_ref.shape[:2]
    half = 32
    for j in range(blocks):
        parts = [parts_ref[i, j].astype(F32) for i in range(count)]
        ms = [p[half + 2 : half + 3] + p[half + 3 : half + 4] for p in parts]
        top = functools.reduce(jnp.maximum, ms)
        acc, total = 0.0, 0.0
        for p, m in zip(parts, ms):
            factor = jnp.exp2(m - top)
            acc = acc + p[:half] * factor
            total = total + (p[half : half + 1] + p[half + 1 : half + 2]) * factor
        out_ref[j] = (acc / total).astype(BF16) if final else pack(acc, total, top)


def combine(parts, final=False):
    vmem = pl.BlockSpec(memory_space=pltpu.VMEM)
    rows = 32 if final else PAY
    return pl.pallas_call(
        functools.partial(combine_kernel, final),
        out_shape=jax.ShapeDtypeStruct((parts.shape[1], rows, 128), BF16),
        in_specs=[vmem],
        out_specs=vmem,
        name="combine",
    )(parts)


def place_kernel(parts_ref, out_ref):
    half = parts_ref.shape[1]
    for i in range(parts_ref.shape[0] // 2):
        one, two = parts_ref[2 * i].astype(F32), parts_ref[2 * i + 1].astype(F32)
        lane = lax.broadcasted_iota(jnp.int32, one.shape, 1)
        low = jnp.where(lane < 64, one, pltpu.roll(two, 64, 1))
        high = jnp.where(lane < 64, pltpu.roll(one, 64, 1), two)
        out_ref[:half, pl.ds(128 * i, 128)] = low.astype(BF16)
        out_ref[half:, pl.ds(128 * i, 128)] = high.astype(BF16)


def place(parts):
    vmem = pl.BlockSpec(memory_space=pltpu.VMEM)
    return pl.pallas_call(
        place_kernel,
        out_shape=jax.ShapeDtypeStruct((64, 64 * parts.shape[0]), BF16),
        in_specs=[vmem],
        out_specs=vmem,
        name="place",
    )(parts)


def exchange(parts, axis):
    return lax.all_to_all(parts, axis, split_axis=0, concat_axis=0, tiled=True)


def spread(block, axis):
    return exchange(jnp.broadcast_to(block[None], (lax.axis_size(axis[0]) * lax.axis_size(axis[1]),) + block.shape), axis)


def body(patches, w_patch, patch_bias, w_kv, queries):
    size = queries.shape[1]
    latents = queries.shape[0]
    tokens = patches.shape[0]
    step = tokens // CHUNKS
    chunks = [
        lax.all_gather(patches[i * step : (i + 1) * step], "z", axis=0, tiled=True)
        for i in range(CHUNKS)
    ]

    weight = w_patch.astype(F32)
    weight = weight - jnp.mean(weight, axis=1, keepdims=True)
    bias = patch_bias - jnp.mean(patch_bias)
    embed = jnp.dot(patches, w_patch, preferred_element_type=F32) + patch_bias
    mean = jnp.mean(embed, axis=-1, keepdims=True)
    var = jnp.mean((embed - mean) * (embed - mean), axis=-1)
    rstd = lax.rsqrt(var + 1e-05)
    rstd = lax.all_gather(rstd.reshape(tokens // 128, 128), "z", axis=0, tiled=False)
    rstd = rstd.reshape(-1, CHUNKS, step)

    w_pair = lax.all_gather(w_kv, "c", axis=0, tiled=False)
    q_pair = lax.all_gather(queries.T, "c", axis=0, tiled=False)
    scale = jnp.where(jnp.arange(2 * size) < size, LOG2E * float(size) ** (-0.5), 1.0)
    fold = jnp.einsum("pd,hdn->phn", weight, w_pair.astype(F32), precision=lax.Precision.HIGHEST)
    fold = (fold * scale).reshape(weight.shape[0], -1).astype(BF16)
    fold_bias = jnp.einsum("d,hdn->hn", bias, w_pair.astype(F32), precision=lax.Precision.HIGHEST)
    fold_bias = (fold_bias * scale).reshape(1, -1)

    state = None
    for i, chunk in enumerate(chunks):
        column = rstd[:, i].reshape(-1, 1)
        state = attend(chunk, column, fold, fold_bias, q_pair, state, i == CHUNKS - 1)

    with jax.named_scope("totals"):
        part = combine(exchange(state, "c"))
        out = combine(exchange(part[:, None], ("y", "x")), final=True)
    with jax.named_scope("readout"):
        return place(spread(out[0], ("y", "x"))).T


def solution(mesh):
    grid = Mesh(mesh.devices.reshape(8, 4, 8, 2), ("y", "x", "z", "c"))
    head = P(None, ("z", "c"))
    placed = (P(("y", "x", "z", "c"), None), P(), P(), head, head)
    return jax.shard_map(body, mesh=grid, in_specs=placed, out_specs=head, check_vma=False)
```

time: 448 us -> 175 us (0.39)
  the two profiles are of different devices: /device:TPU:64 before, /device:TPU:8 now
where the time goes in v1:
time: 175 us
  blocking collectives  79.4 us (45%)
  Pallas kernels  42.1 us (24%)
  waiting for transfers between devices  29.3 us (17%)
  between operations  14.1 us (8%)
  local copies, waits for them, and re-layouts  4.52 us (3%)
  matrix products  3.18 us (2%)
  other arithmetic  1.88 us (1%)
    all_to_all x3, blocking collectives, exchange(): return lax.all_to_all(parts, axis, split_axis=0, concat_axis=0, tiled=True)  47.5 us
    pallas_call x1, Pallas kernels, attend(): pl.pallas_call(functools.partial(attend_kernel, first, last, block), out_...  36.5 us
    all_gather x1, waiting for transfers between devices, body(): lax.all_gather(patches[i * step:(i + 1) * step], 'z', axis=0, tiled=True)  28.6 us
    all_gather x1, blocking collectives, body(): lax.all_gather(rstd.reshape(tokens // 128, 128), 'z', axis=0, tiled=False)  27.2 us
    pallas_call x2, Pallas kernels, combine(): pl.pallas_call(functools.partial(combine_kernel, final), out_shape=jax.Sh...  3.83 us
  transfers between devices with their start and end apart: 1, of which 1 were waited for; matrix products, arithmetic and copies ran while one was open for 5% of the time, Pallas kernels for 0%

profile of v1, /device:TPU:8, one launch (start us, length us, event | category | flops | bytes accessed | tf_op | source)
XLA Modules:
  0.0 174.5 jit_solution(10103756820941861171)
XLA Ops:
  6.5 0.0 copy-start
  6.5 0.0 all-gather.4.cloned.1.call-start
  6.5 0.7 all-gather.4.cloned.1.call-update
  7.3 2.4 %all-gather = bf16[2048,128]{1,0:T(8,128)(2,1)S(1)} all-gather(bf16[1024,128]{1,0:T(8,128)(2,1)} %param.8), channel_id=2, replica_groups=mesh['y'=8,'x'=4,'z'=8,'c'=2] {'c'}, dimensions={0}, use_global_device_ids=true | all-gather | bytes 786432 | tf_op jit(solution)/shard_map/all_gather | solution.py:249
  9.7 0.2 copy.10
  9.9 0.0 copy-done
  9.9 0.3 convert_reduce_fusion
  10.2 2.0 %fusion = f32[768,256]{0,1:S(1)} fusion(bf16[1024,256]{0,1:T(8,128)(2,1)S(1)} %bitcast.29, bf16[768,1024]{1,0:T(8,128)(2,1)S(1)} %copy-done, f32[768]{0:T(1024)S(1)} %broadcast_multiply_fusion), kind=kOutput, calls=%fused_computation.2 | convolution fusion | flops 2417491968 | bytes 2886656
  12.2 0.0 copy-start.3
  12.2 0.0 copy-start.1
  12.2 0.1 multiply_convert_fusion
  12.3 0.9 copy.14.refs_2_
  13.2 0.0 copy-done.3
  13.2 0.6 reduce_sum.39
  13.8 0.0 copy-done.1
  13.8 0.9 fusion.2
  14.7 0.0 copy-start.2
  14.7 0.3 multiply_reduce_fusion
  15.0 27.2 %all_gather.19 = f32[8,3,128]{2,1,0:T(4,128)S(1)} all-gather(f32[1,3,128]{2,1,0:T(4,128)S(1)} %rsqrt_bitcast_fusion), channel_id=1, replica_groups=mesh['y'=8,'x'=4,'z'=8,'c'=2] {'z'}, dimensions={0}, use_global_device_ids=true | all-gather | bytes 13824 | tf_op jit(solution)/shard_map/all_gather | solution.py:246
  42.3 2.6 %reshape_squeeze_reshape.4.refs_1_ = f32[3072,1]{1,0:T(8,128)} reshape(f32[8,3,128]{2,1,0:T(4,128)S(1)} %all_gather.19) | data formatting | bytes 24576 | tf_op jit(solution)/shard_map/reshape;squeeze;reshape | solution.py:259
  45.5 0.0 copy-done.2
  45.6 2.3 %all-gather.1 = bf16[128,2048]{1,0:T(8,128)(2,1)} all-gather(bf16[64,2048]{1,0:T(8,128)(2,1)S(1)} %bitcast.30), channel_id=3, replica_groups=mesh['y'=8,'x'=4,'z'=8,'c'=2] {'c'}, dimensions={0}, use_global_device_ids=true | all-gather | bytes 786432 | tf_op jit(solution)/shard_map/all_gather | solution.py:250
  47.9 0.3 fusion.3
  48.2 0.6 broadcast_multiply_fusion.2
  48.8 28.6 %all-gather.4.cloned.1.call-done.refs_0_ = bf16[3072,768]{1,0:T(8,128)(2,1)} async-done(((bf16[384,768]{1,0:T(8,128)(2,1)}), bf16[3072,768]{1,0:T(8,128)(2,1)}) %all-gather.4.cloned.1.call-update) | async-done | bytes 4718608 | tf_op jit(solution)/shard_map/all_gather | solution.py:235
  77.4 36.5 %attend.1 = bf16[2,32,48,128]{3,2,1,0:T(8,128)(2,1)} custom-call(bf16[3072,768]{1,0:T(8,128)(2,1)} %all-gather.4.cloned.1.call-done.refs_0_, f32[3072,1]{1,0:T(8,128)} %reshape_squeeze_reshape.4.refs_1_, bf16[768,256]{1,0:T(8,128)(2,1)} %copy.14.refs_2_, f32[1,256]{1,0:T(1,128)} %bitcast.34, bf16[2,64,2048]{2,1,0:T(8,128)(2,1)} %bitcast.28), custom_call_target="tpu_custom_call" | custom-call | flops 12884901888 | bytes 4718592 | tf_op jit(solution)/shard_map/attend/pallas_call | solution.py:158
  113.8 6.3 %all_to_all.15.parts_ref = bf16[2,32,48,128]{3,2,1,0:T(8,128)(2,1)} all-to-all(bf16[2,32,48,128]{3,2,1,0:T(8,128)(2,1)} %attend.1), channel_id=1, replica_groups=mesh['y'=8,'x'=4,'z'=8,'c'=2] {'c'}, dimensions={0} | all-to-all | bytes 1572864 | tf_op jit(solution)/shard_map/totals/all_to_all | solution.py:222
  120.2 2.1 %combine.2 = bf16[32,48,128]{2,1,0:T(8,128)(2,1)} custom-call(bf16[2,32,48,128]{3,2,1,0:T(8,128)(2,1)} %all_to_all.15.parts_ref), custom_call_target="tpu_custom_call" | custom-call | tf_op jit(solution)/shard_map/totals/combine/pallas_call | solution.py:190
  122.3 25.0 %all_to_all.16.parts_ref = bf16[32,1,48,128]{3,2,1,0:T(8,128)(2,1)} all-to-all(bf16[32,1,48,128]{3,2,1,0:T(8,128)(2,1)} %bitcast.26), channel_id=1, replica_groups=mesh['y'=8,'x'=4,'z'=8,'c'=2] {'y','x'}, dimensions={0} | all-to-all | bytes 786432 | tf_op jit(solution)/shard_map/totals/all_to_all | solution.py:222
  147.3 1.7 combine.3
  149.0 0.7 broadcast_in_dim.27
  149.7 16.2 %all_to_all.17.parts_ref = bf16[32,32,128]{2,1,0:T(8,128)(2,1)} all-to-all(bf16[32,32,128]{2,1,0:T(8,128)(2,1)S(1)} %broadcast_in_dim.27), channel_id=1, replica_groups=mesh['y'=8,'x'=4,'z'=8,'c'=2] {'y','x'}, dimensions={0} | all-to-all | bytes 524288 | tf_op jit(solution)/shard_map/readout/all_to_all | solution.py:222
  165.9 1.8 %place.1 = bf16[64,2048]{1,0:T(8,128)(2,1)} custom-call(bf16[32,32,128]{2,1,0:T(8,128)(2,1)} %all_to_all.17.parts_ref), custom_call_target="tpu_custom_call" | custom-call | tf_op jit(solution)/shard_map/readout/place/pallas_call | solution.py:212
  (5 shorter events, 0.0 us)
Async XLA Ops:
  6.5 3.3 %copy-start = (bf16[768,1024]{1,0:T(8,128)(2,1)S(1)}, bf16[768,1024]{1,0:T(8,128)(2,1)}, u32[]{:S(2)}) copy-start(bf16[768,1024]{1,0:T(8,128)(2,1)} %param.6) | copy-start | bytes 4718596
  6.5 70.8 %all-gather.4.cloned.1.call-start = ((), (), s32[]{:S(2)}) async-start(), calls=%async_computation.3 | async-start | bytes 5308416 | tf_op jit(solution)/shard_map/all_gather | solution.py:235
  12.2 1.1 copy-start.3
  12.2 1.6 copy-start.1
  14.7 30.8 %copy-start.2 = (bf16[2048,64]{0,1:T(8,128)(2,1)S(1)}, bf16[2048,64]{0,1:T(8,128)(2,1)}, u32[]{:S(2)}) copy-start(bf16[2048,64]{0,1:T(8,128)(2,1)} %param.9) | copy-start | bytes 786436
Sparse Core Ops, SparseCore 0:
  9.4 67.8 all-gather.3

commit v2 on v1

v2 whole, which is shorter than its diff:
```python
import functools

import jax
import jax.numpy as jnp
from jax import lax
from jax.experimental import pallas as pl
from jax.experimental.pallas import tpu as pltpu
from jax.sharding import Mesh
from jax.sharding import PartitionSpec as P

F32 = jnp.float32
BF16 = jnp.bfloat16
LOG2E = 1.4426950408889634
LIMIT = 2.0**64
RING = 128
BLOCK = 1024
ROWS = 80
PAY = 48
PLAIN = (((1,), (0,)), ((), ()))


def split(value):
    high = value.astype(BF16)
    return high, (value - high.astype(F32)).astype(BF16)


def attend_kernel(pieces, heads, first, last, *refs):
    xs, refs = refs[:pieces], refs[pieces:]
    rstd_ref, w_ref, b_ref, q_ref = refs[:4]
    refs = refs[4:]
    if not first:
        acc_ins, m_ins, refs = refs[:heads], refs[heads : 2 * heads], refs[2 * heads :]
    if last:
        pay_ref, refs = refs[0], refs[1:]
    acc_refs, m_refs, refs = refs[:heads], refs[heads : 2 * heads], refs[2 * heads :]
    k_ref, v_ref, qa_ref = refs
    tokens = k_ref.shape[1]
    _, size, latents = q_ref.shape
    block = min(BLOCK, tokens)
    steps = tokens // block

    def project(x, start, count):
        kv = jnp.dot(x, w_ref[...], preferred_element_type=F32)
        kv = (kv + b_ref[...]) * rstd_ref[pl.ds(start, count), :]
        lane = lax.broadcasted_iota(jnp.int32, (count, 2 * size), 1)
        for h in range(heads):
            mine = kv[:, 2 * size * h : 2 * size * (h + 1)]
            k_ref[h, pl.ds(start, count), :] = jnp.where(lane < size, mine, 1.0).astype(BF16)
            v_ref[h, :size, pl.ds(start, count)] = mine.T[size:, :].astype(BF16)

    start = 0
    for x_ref in xs:
        count = min(512, x_ref.shape[0])
        for t in range(x_ref.shape[0] // count):
            project(x_ref[pl.ds(t * count, count), :], start, count)
            start += count

    def scores(h, keys):
        return lax.dot_general(k_ref[h, keys, :], qa_ref[h], PLAIN, preferred_element_type=F32)

    def set_max(h, value):
        high, low = split(value)
        m_refs[h][...] = high.astype(F32) + low.astype(F32)
        qa_ref[h, size : size + 16, :] = jnp.concatenate(
            [-high, -low, jnp.zeros((14, latents), BF16)], axis=0
        )

    for h in range(heads):
        v_ref[h, size:, :] = jnp.ones((ROWS - size, tokens), BF16)
        qa_ref[h, :size, :] = q_ref[h]
        qa_ref[h, size:, :] = jnp.zeros((size, latents), BF16)
        if first:
            set_max(h, jnp.max(scores(h, pl.ds(0, 128)), axis=0, keepdims=True))
        else:
            set_max(h, m_ins[h][...])

    def add(h, keys):
        probs = jnp.exp2(scores(h, keys)).astype(BF16)
        acc_refs[h][...] += lax.dot_general(v_ref[h, :, keys], probs, PLAIN, preferred_element_type=F32)

    for h in range(heads):
        acc_ref, m_ref = acc_refs[h], m_refs[h]
        acc_ref[...] = jnp.zeros((ROWS, latents), F32) if first else acc_ins[h][...]
        for t in range(steps):
            add(h, pl.ds(t * block, block))

        @pl.when(jnp.logical_not(jnp.max(acc_ref[size : size + 8, :]) < LIMIT))
        def _(h=h, acc_ref=acc_ref, m_ref=m_ref):
            before = m_ref[...]
            qa_ref[h, size:, :] = jnp.zeros((size, latents), BF16)

            def at(t):
                return pl.ds(pl.multiple_of(t * block, block), block)

            def widen(t, best):
                return jnp.maximum(best, jnp.max(scores(h, at(t)), axis=0, keepdims=True))

            set_max(h, lax.fori_loop(0, steps, widen, before))
            if first:
                acc_ref[...] = jnp.zeros((ROWS, latents), F32)
            else:
                acc_ref[...] = acc_ins[h][...] * jnp.exp2(before - m_ref[...])

            def redo(t, carry):
                add(h, at(t))
                return carry

            lax.fori_loop(0, steps, redo, 0)

        if last:
            for i in range(latents // 128):
                lanes = pl.ds(128 * i, 128)
                acc, total, m = acc_ref[:size, lanes], acc_ref[size : size + 1, lanes], m_ref[:, lanes]
                for side in range(2):
                    pay_ref[2 * i + side] = pack(fold_half(acc, side), both(total, side), both(m, side))


def both(row, side):
    lane = lax.broadcasted_iota(jnp.int32, row.shape, 1)
    keep = lane < 64 if side == 0 else lane >= 64
    return jnp.where(keep, row, pltpu.roll(row, 64, 1))


def fold_half(acc, side):
    half = acc.shape[0] // 2
    low, high = acc[:half], acc[half:]
    if side == 0:
        high = pltpu.roll(high, 64, 1)
    else:
        low = pltpu.roll(low, 64, 1)
    lane = lax.broadcasted_iota(jnp.int32, low.shape, 1)
    return jnp.where(lane < 64, low, high)


def pack(acc, total, m):
    t_high, m_high = total.astype(BF16).astype(F32), m.astype(BF16).astype(F32)
    fill = jnp.zeros((PAY - acc.shape[0] - 4, acc.shape[1]), F32)
    rows = [acc, t_high, total - t_high, m_high, m - m_high, fill]
    return jnp.concatenate(rows, axis=0).astype(BF16)


def attend(xs, rstd, w, b, q, state, last):
    heads, size, latents = q.shape
    tokens = sum(x.shape[0] for x in xs)
    first = state is None
    vmem = pl.BlockSpec(memory_space=pltpu.VMEM)
    accs = [jax.ShapeDtypeStruct((ROWS, latents), F32)] * heads
    ms = [jax.ShapeDtypeStruct((1, latents), F32)] * heads
    scratch = [
        pltpu.VMEM((heads, tokens, 2 * size), BF16),
        pltpu.VMEM((heads, ROWS, tokens), BF16),
        pltpu.VMEM((heads, 2 * size, latents), BF16),
    ]
    if last:
        out = jax.ShapeDtypeStruct((latents // 64, PAY, 128), BF16)
        scratch = [pltpu.VMEM(i.shape, F32) for i in accs + ms] + scratch
    else:
        out = accs + ms
    ins = (*xs, rstd, w, b, q) + (() if first else tuple(state))
    work = tokens * latents * heads
    return pl.pallas_call(
        functools.partial(attend_kernel, len(xs), heads, first, last),
        out_shape=out,
        in_specs=[vmem] * len(ins),
        out_specs=jax.tree.map(lambda _: vmem, out),
        scratch_shapes=scratch,
        compiler_params=pltpu.CompilerParams(vmem_limit_bytes=56 << 20),
        cost_estimate=pl.CostEstimate(
            flops=16 * work * size, bytes_accessed=tokens * w.shape[0] * 2, transcendentals=work
        ),
        name="attend",
    )(*ins)


def combine_kernel(final, parts_ref, out_ref):
    count, blocks = parts_ref.shape[:2]
    half = 32
    for j in range(blocks):
        parts = [parts_ref[i, j].astype(F32) for i in range(count)]
        ms = [p[half + 2 : half + 3] + p[half + 3 : half + 4] for p in parts]
        top = functools.reduce(jnp.maximum, ms)
        acc, total = 0.0, 0.0
        for p, m in zip(parts, ms):
            factor = jnp.exp2(m - top)
            acc = acc + p[:half] * factor
            total = total + (p[half : half + 1] + p[half + 1 : half + 2]) * factor
        out_ref[j] = (acc / total).astype(BF16) if final else pack(acc, total, top)


def combine(parts, final=False):
    vmem = pl.BlockSpec(memory_space=pltpu.VMEM)
    rows = 32 if final else PAY
    return pl.pallas_call(
        functools.partial(combine_kernel, final),
        out_shape=jax.ShapeDtypeStruct((parts.shape[1], rows, 128), BF16),
        in_specs=[vmem],
        out_specs=vmem,
        name="combine",
    )(parts)


def place_kernel(parts_ref, out_ref):
    half = parts_ref.shape[1]
    for i in range(parts_ref.shape[0] // 2):
        one, two = parts_ref[2 * i].astype(F32), parts_ref[2 * i + 1].astype(F32)
        lane = lax.broadcasted_iota(jnp.int32, one.shape, 1)
        low = jnp.where(lane < 64, one, pltpu.roll(two, 64, 1))
        high = jnp.where(lane < 64, pltpu.roll(one, 64, 1), two)
        out_ref[:half, pl.ds(128 * i, 128)] = low.astype(BF16)
        out_ref[half:, pl.ds(128 * i, 128)] = high.astype(BF16)


def place(parts):
    vmem = pl.BlockSpec(memory_space=pltpu.VMEM)
    return pl.pallas_call(
        place_kernel,
        out_shape=jax.ShapeDtypeStruct((64, 64 * parts.shape[0]), BF16),
        in_specs=[vmem],
        out_specs=vmem,
        name="place",
    )(parts)


def exchange(parts, axis):
    return lax.all_to_all(parts, axis, split_axis=0, concat_axis=0, tiled=True)


def spread(block, axis):
    return exchange(jnp.broadcast_to(block[None], (lax.axis_size(axis[0]) * lax.axis_size(axis[1]),) + block.shape), axis)


def shift(block, axis, by):
    size = lax.axis_size(axis)
    return lax.ppermute(block, axis, [(i, (i + by) % size) for i in range(size)])


def ring(block):
    half = block.shape[0] // 2
    blocks, up, down = [block], block, block
    for _ in range(3):
        up, down = shift(up, "z", 1), shift(down, "z", -1)
        blocks += [up, down]
    last = [shift(up[:half], "z", 1), shift(down[half:], "z", -1)]
    return blocks + [jnp.concatenate(last, axis=0)]


def body(patches, w_patch, patch_bias, w_kv, queries):
    size = queries.shape[1]
    tokens = patches.shape[0]
    rest = lax.all_gather(patches[RING:], "z", axis=0, tiled=True)
    blocks = ring(patches[:RING])

    weight = w_patch.astype(F32)
    weight = weight - jnp.mean(weight, axis=1, keepdims=True)
    bias = patch_bias - jnp.mean(patch_bias)
    embed = jnp.dot(patches, w_patch, preferred_element_type=F32) + patch_bias
    mean = jnp.mean(embed, axis=-1, keepdims=True)
    var = jnp.mean((embed - mean) * (embed - mean), axis=-1)
    rstd = lax.rsqrt(var + 1e-05)
    rstd = lax.all_gather(rstd.reshape(tokens // 128, 128), "z", axis=0, tiled=False)
    rstd = rstd.reshape(-1, tokens)
    turned = jnp.concatenate([rstd, rstd])[:, :RING]
    turned = lax.dynamic_slice_in_dim(turned, lax.axis_index("z"), 8, axis=0)
    order = [0, 7, 1, 6, 2, 5, 3, 4]
    rstd_ring = jnp.concatenate([turned[i : i + 1] for i in order]).reshape(-1, 1)
    rstd_rest = rstd[:, RING:].reshape(-1, 1)

    w_pair = jnp.stack([shift(w_kv, "c", 1), w_kv])
    q_pair = jnp.stack([shift(queries.T, "c", 1), queries.T])
    scale = jnp.where(jnp.arange(2 * size) < size, LOG2E * float(size) ** (-0.5), 1.0)
    fold = jnp.einsum("pd,hdn->hpn", weight, w_pair.astype(F32), precision=lax.Precision.HIGHEST)
    fold = (fold * scale).astype(BF16)
    fold_bias = jnp.einsum("d,hdn->hn", bias, w_pair.astype(F32), precision=lax.Precision.HIGHEST)
    fold_bias = fold_bias * scale

    state = attend(
        blocks, rstd_ring, jnp.concatenate([fold[0], fold[1]], axis=1),
        fold_bias.reshape(1, -1), q_pair, None, False,
    )
    pays = [
        attend(
            [rest], rstd_rest, fold[h], fold_bias[h][None], q_pair[h : h + 1],
            (state[h], state[2 + h]), True,
        )
        for h in range(2)
    ]

    with jax.named_scope("totals"):
        part = combine(jnp.stack([shift(pays[0], "c", 1), pays[1]]))
        out = combine(exchange(part[:, None], ("y", "x")), final=True)
    with jax.named_scope("readout"):
        return place(spread(out[0], ("y", "x"))).T


def solution(mesh):
    grid = Mesh(mesh.devices.reshape(8, 4, 8, 2), ("y", "x", "z", "c"))
    head = P(None, ("z", "c"))
    placed = (P(("y", "x", "z", "c"), None), P(), P(), head, head)
    return jax.shard_map(body, mesh=grid, in_specs=placed, out_specs=head, check_vma=False)
```

time: 175 us -> 185 us (1.057)
  the two profiles are of different devices: /device:TPU:8 before, /device:TPU:64 now
where the time goes in v2:
time: 185 us
  blocking collectives  65.3 us (35%)
  Pallas kernels  49 us (26%)
  starting transfers between devices  34 us (18%)
  between operations  14.5 us (8%)
  local copies, waits for them, and re-layouts  6.8 us (4%)
  other arithmetic  5.63 us (3%)
  waiting for transfers between devices  5.24 us (3%)
  matrix products  4.2 us (2%)
    pallas_call x3, Pallas kernels, attend(): pl.pallas_call(functools.partial(attend_kernel, len(xs), heads, first, la...  43.4 us
    all_to_all x2, blocking collectives, exchange(): return lax.all_to_all(parts, axis, split_axis=0, concat_axis=0, tiled=True)  42.2 us
    ppermute x11, starting transfers between devices, shift(): lax.ppermute(block, axis, [(i, (i + by) % size) for i in range(size)])  33.9 us
    all_gather x1, blocking collectives, body(): lax.all_gather(rstd.reshape(tokens // 128, 128), 'z', axis=0, tiled=False)  23.1 us
    ppermute x11, waiting for transfers between devices, shift(): lax.ppermute(block, axis, [(i, (i + by) % size) for i in range(size)])  5.2 us
    pallas_call x2, Pallas kernels, combine(): pl.pallas_call(functools.partial(combine_kernel, final), out_shape=jax.Sh...  3.85 us
  transfers between devices with their start and end apart: 12, of which 3 were waited for; matrix products, arithmetic and copies ran while one was open for 6% of the time, Pallas kernels for 16%

profile of v2, /device:TPU:64, one launch (start us, length us, event | category | flops | bytes accessed | tf_op | source)
XLA Modules:
  0.0 184.6 jit_solution(7020963556395661368)
XLA Ops:
  6.5 0.0 all-gather.2.cloned.1.call-start
  6.6 1.9 %slice.55 = bf16[256,768]{1,0:T(8,128)(2,1)} slice(bf16[384,768]{1,0:T(8,128)(2,1)} %param.5), slice={[128:384], [0:768]} | slice | bytes 786432 | tf_op jit(solution)/shard_map/slice | solution.py:250
  8.5 0.0 all-gather.2.cloned.1.call-update
  8.5 0.9 slice.59.refs_0_
  9.5 0.0 copy-start.6
  9.5 4.3 %collective-permute-start.2 = (bf16[128,768]{1,0:T(8,128)(2,1)S(1)}, bf16[128,768]{1,0:T(8,128)(2,1)S(1)}, u32[]{:S(2)}, u32[]{:S(2)}) collective-permute-start(bf16[128,768]{1,0:T(8,128)(2,1)S(1)} %slice.59.refs_0_), channel_id=1, source_target_pairs={{0,2},{2,4},{4,6},{6,8},{8,10},{10,12},{12,14},{14,0},{1,3},{3,5},... | collective-permute-start | bytes 589832 | tf_op jit(solution)/shard_map/ppermute | solution.py:234
  13.8 4.6 %collective-permute-start.3 = (bf16[128,768]{1,0:T(8,128)(2,1)S(1)}, bf16[128,768]{1,0:T(8,128)(2,1)S(1)}, u32[]{:S(2)}, u32[]{:S(2)}) collective-permute-start(bf16[128,768]{1,0:T(8,128)(2,1)S(1)} %slice.59.refs_0_), channel_id=1, source_target_pairs={{0,14},{2,0},{4,2},{6,4},{8,6},{10,8},{12,10},{14,12},{1,15},{3,1}... | collective-permute-start | bytes 589832 | tf_op jit(solution)/shard_map/ppermute | solution.py:234
  18.4 0.0 copy-done.3
  18.4 0.1 copy.21
  18.5 1.9 %collective-permute-start = (bf16[1024,128]{0,1:T(8,128)(2,1)S(1)}, bf16[1024,128]{0,1:T(8,128)(2,1)S(1)}, u32[]{:S(2)}, u32[]{:S(2)}) collective-permute-start(bf16[1024,128]{0,1:T(8,128)(2,1)S(1)} %copy.21), channel_id=1, source_target_pairs={{0,1},{1,0},{2,3},{3,2},{4,5},{5,4},{6,7},{7,6},{8,9},{9,8},{10,11... | collective-permute-start | bytes 786440 | tf_op jit(solution)/shard_map/ppermute | solution.py:234
  20.4 0.0 copy-done.4
  20.5 2.4 %collective-permute-start.1 = (bf16[64,2048]{1,0:T(8,128)(2,1)S(1)}, bf16[64,2048]{1,0:T(8,128)(2,1)S(1)}, u32[]{:S(2)}, u32[]{:S(2)}) collective-permute-start(bf16[64,2048]{1,0:T(8,128)(2,1)S(1)} %bitcast.57), channel_id=1, source_target_pairs={{0,1},{1,0},{2,3},{3,2},{4,5},{5,4},{6,7},{7,6},{8,9},{9,8},{10,11... | collective-permute-start | bytes 786440 | tf_op jit(solution)/shard_map/ppermute | solution.py:234
  22.9 0.0 copy-done
  22.9 0.0 copy-done.9
  22.9 1.9 %fusion.16 = (f32[384]{0:T(512)S(1)}, f32[384,1024]{1,0:T(8,128)S(1)}) fusion(f32[1024]{0:T(1024)S(1)} %copy-done.9, bf16[384,768]{1,0:T(8,128)(2,1)} %param.5, bf16[768,1024]{1,0:T(8,128)(2,1)S(1)} %copy-done), kind=kOutput, calls=%fused_computation.30 | convolution fusion | flops 604765824 | bytes 3741184 | tf_op jit(solution)/shard_map/dot_general | solution.py:256
  24.8 0.3 multiply_reduce_fusion
  25.2 23.1 %all_gather.7 = f32[8,3,128]{2,1,0:T(4,128)S(1)} all-gather(f32[1,3,128]{2,1,0:T(4,128)S(1)} %rsqrt_bitcast_fusion), channel_id=1, replica_groups=mesh['y'=8,'x'=4,'z'=8,'c'=2] {'z'}, dimensions={0}, use_global_device_ids=true | all-gather | bytes 13824 | tf_op jit(solution)/shard_map/all_gather | solution.py:260
  48.3 0.6 reduce_sum.39
  49.5 0.3 convert_reduce_fusion
  49.9 1.0 copy.24.refs_8_
  50.9 1.4 copy.30
  52.3 0.0 collective-permute-done.2.refs_1_
  52.3 4.2 %collective-permute-start.4 = (bf16[128,768]{1,0:T(8,128)(2,1)S(1)}, bf16[128,768]{1,0:T(8,128)(2,1)S(1)}, u32[]{:S(2)}, u32[]{:S(2)}) collective-permute-start(bf16[128,768]{1,0:T(8,128)(2,1)S(1)} %collective-permute-done.2.refs_1_), channel_id=1, source_target_pairs={{0,2},{2,4},{4,6},{6,8},{8,10},{10,12},{12,14},{14,0},{1,3},{3,5},... | collective-permute-start | bytes 589832 | tf_op jit(solution)/shard_map/ppermute | solution.py:234
  56.5 0.0 collective-permute-done.3.refs_2_
  56.5 0.0 copy-start.12
  56.5 1.9 %collective-permute-start.5 = (bf16[128,768]{1,0:T(8,128)(2,1)S(1)}, bf16[128,768]{1,0:T(8,128)(2,1)S(1)}, u32[]{:S(2)}, u32[]{:S(2)}) collective-permute-start(bf16[128,768]{1,0:T(8,128)(2,1)S(1)} %collective-permute-done.3.refs_2_), channel_id=1, source_target_pairs={{0,14},{2,0},{4,2},{6,4},{8,6},{10,8},{12,10},{14,12},{1,15},{3,1}... | collective-permute-start | bytes 589832 | tf_op jit(solution)/shard_map/ppermute | solution.py:234
  58.4 0.0 collective-permute-done
  58.4 0.1 pad_maximum_fusion.1
  58.5 0.0 collective-permute-done.1
  58.5 0.0 copy-start.5
  58.5 0.9 pad_maximum_fusion.2.refs_11_
  59.4 0.5 fusion.17
  59.9 1.8 fusion.10
  61.7 0.0 copy-done.11
  61.7 0.0 copy-done.12
  61.7 0.0 copy-done.5
  61.8 2.6 %collective-permute-done.4.refs_3_ = bf16[128,768]{1,0:T(8,128)(2,1)S(1)} collective-permute-done((bf16[128,768]{1,0:T(8,128)(2,1)S(1)}, bf16[128,768]{1,0:T(8,128)(2,1)S(1)}, u32[]{:S(2)}, u32[]{:S(2)}) %collective-permute-start.4) | collective-permute-done | bytes 196640 | tf_op jit(solution)/shard_map/ppermute | solution.py:234
  64.4 2.3 %collective-permute-start.6 = (bf16[128,768]{1,0:T(8,128)(2,1)S(1)}, bf16[128,768]{1,0:T(8,128)(2,1)S(1)}, u32[]{:S(2)}, u32[]{:S(2)}) collective-permute-start(bf16[128,768]{1,0:T(8,128)(2,1)S(1)} %collective-permute-done.4.refs_3_), channel_id=1, source_target_pairs={{0,2},{2,4},{4,6},{6,8},{8,10},{10,12},{12,14},{14,0},{1,3},{3,5},... | collective-permute-start | bytes 589832 | tf_op jit(solution)/shard_map/ppermute | solution.py:234
  66.7 0.0 collective-permute-done.5.refs_4_
  66.7 3.6 %collective-permute-start.7 = (bf16[128,768]{1,0:T(8,128)(2,1)S(1)}, bf16[128,768]{1,0:T(8,128)(2,1)S(1)}, u32[]{:S(2)}, u32[]{:S(2)}) collective-permute-start(bf16[128,768]{1,0:T(8,128)(2,1)S(1)} %collective-permute-done.5.refs_4_), channel_id=1, source_target_pairs={{0,14},{2,0},{4,2},{6,4},{8,6},{10,8},{12,10},{14,12},{1,15},{3,1}... | collective-permute-start | bytes 589832 | tf_op jit(solution)/shard_map/ppermute | solution.py:234
  70.3 0.5 fusion.15
  70.8 1.2 collective-permute-done.6.refs_5_
  72.0 2.3 %collective-permute-start.8 = (bf16[64,768]{1,0:T(8,128)(2,1)S(1)}, bf16[64,768]{1,0:T(8,128)(2,1)S(1)}, u32[]{:S(2)}, u32[]{:S(2)}) collective-permute-start(bf16[64,768]{1,0:T(8,128)(2,1)S(1)} %slice.74), channel_id=1, source_target_pairs={{0,2},{2,4},{4,6},{6,8},{8,10},{10,12},{12,14},{14,0},{1,3},{3,5},... | collective-permute-start | bytes 294920 | tf_op jit(solution)/shard_map/ppermute | solution.py:234
  74.3 0.0 collective-permute-done.7.refs_6_
  74.3 4.4 %collective-permute-start.9 = (bf16[64,768]{1,0:T(8,128)(2,1)S(1)}, bf16[64,768]{1,0:T(8,128)(2,1)S(1)}, u32[]{:S(2)}, u32[]{:S(2)}) collective-permute-start(bf16[64,768]{1,0:T(8,128)(2,1)S(1)} %slice.75), channel_id=1, source_target_pairs={{0,14},{2,0},{4,2},{6,4},{8,6},{10,8},{12,10},{14,12},{1,15},{3,1}... | collective-permute-start | bytes 294920 | tf_op jit(solution)/shard_map/ppermute | solution.py:234
  78.8 0.8 pad_maximum_fusion.3.refs_9_
  79.6 0.0 collective-permute-done.8
  79.6 1.4 collective-permute-done.9
  81.0 0.7 pad_maximum_fusion.4.refs_7_
  81.7 0.0 copy-done.14
  81.7 14.1 %attend.3 = (f32[80,2048]{1,0:T(8,128)}, f32[80,2048]{1,0:T(8,128)}, f32[1,2048]{1,0:T(1,128)}, f32[1,2048]{1,0:T(1,128)}) custom-call(bf16[128,768]{1,0:T(8,128)(2,1)} %copy-done.6, bf16[128,768]{1,0:T(8,128)(2,1)} %copy-done.11, bf16[128,768]{1,0:T(8,128)(2,1)} %copy-done.12, bf16[128,768]{1,0:T(8,128)(2,1)} %copy-done.13, bf16[128,768]{1,0:T(8,128)(2,1)} %copy-done.14, ...), custom_call_target="tpu_custom_call" | custom-call | flops 4294967296 | bytes 1572864 | tf_op jit(solution)/shard_map/attend/pallas_call | solution.py:161
  95.8 0.0 copy-done.1
  95.8 0.0 all-gather.2.cloned.1.call-done.refs_0_
  95.8 14.6 %attend.4 = bf16[32,48,128]{2,1,0:T(8,128)(2,1)} custom-call(bf16[2048,768]{1,0:T(8,128)(2,1)} %all-gather.2.cloned.1.call-done.refs_0_, f32[2048,1]{1,0:T(8,128)} %bitcast.50, bf16[768,128]{1,0:T(8,128)(2,1)} %copy-done.2, f32[1,128]{1,0:T(1,128)} %get-tuple-element.21.refs_3_, bf16[1,64,2048]{2,1,0:T(8,128)(2,1)} %bitcast.60, ...), custom_call_target="tpu_custom_call" | custom-call | flops 4294967296 | bytes 3145728 | tf_op jit(solution)/shard_map/attend/pallas_call | solution.py:161
  110.5 2.1 %collective-permute-start.10 = (bf16[32,48,128]{2,1,0:T(8,128)(2,1)}, bf16[32,48,128]{2,1,0:T(8,128)(2,1)S(1)}, u32[]{:S(2)}, u32[]{:S(2)}) collective-permute-start(bf16[32,48,128]{2,1,0:T(8,128)(2,1)} %attend.4), channel_id=1, source_target_pairs={{0,1},{1,0},{2,3},{3,2},{4,5},{5,4},{6,7},{7,6},{8,9},{9,8},{10,11... | collective-permute-start | bytes 1179656 | tf_op jit(solution)/shard_map/totals/ppermute | solution.py:234
  112.6 14.6 %attend.5 = bf16[32,48,128]{2,1,0:T(8,128)(2,1)} custom-call(bf16[2048,768]{1,0:T(8,128)(2,1)} %all-gather.2.cloned.1.call-done.refs_0_, f32[2048,1]{1,0:T(8,128)} %bitcast.51, bf16[768,128]{1,0:T(8,128)(2,1)} %copy-done.1, f32[1,128]{1,0:T(1,128)} %get-tuple-element.22.refs_3_, bf16[1,64,2048]{2,1,0:T(8,128)(2,1)} %bitcast.56, ...), custom_call_target="tpu_custom_call" | custom-call | flops 4294967296 | bytes 3145728 | tf_op jit(solution)/shard_map/attend/pallas_call | solution.py:161
  127.2 0.0 collective-permute-done.10
  127.2 2.0 %pad_maximum_fusion.parts_ref = bf16[2,32,48,128]{3,2,1,0:T(8,128)(2,1)} fusion(bf16[1,32,48,128]{3,2,1,0:T(8,128)(2,1)} %bitcast.55, bf16[1,32,48,128]{3,2,1,0:T(8,128)(2,1)S(1)} %bitcast.54), kind=kLoop, calls=%fused_computation.10 | loop fusion | flops 393216 | bytes 1572864 | tf_op jit(solution)/shard_map/totals/stack | solution.py:289
  129.2 2.1 %combine.2 = bf16[32,48,128]{2,1,0:T(8,128)(2,1)} custom-call(bf16[2,32,48,128]{3,2,1,0:T(8,128)(2,1)} %pad_maximum_fusion.parts_ref), custom_call_target="tpu_custom_call" | custom-call | tf_op jit(solution)/shard_map/totals/combine/pallas_call | solution.py:193
  131.3 25.6 %all_to_all.10.parts_ref = bf16[32,1,48,128]{3,2,1,0:T(8,128)(2,1)} all-to-all(bf16[32,1,48,128]{3,2,1,0:T(8,128)(2,1)} %bitcast.49), channel_id=1, replica_groups=mesh['y'=8,'x'=4,'z'=8,'c'=2] {'y','x'}, dimensions={0} | all-to-all | bytes 786432 | tf_op jit(solution)/shard_map/totals/all_to_all | solution.py:225
  157.0 1.7 combine.3
  158.7 0.7 broadcast_in_dim.27
  159.4 16.5 %all_to_all.11.parts_ref = bf16[32,32,128]{2,1,0:T(8,128)(2,1)} all-to-all(bf16[32,32,128]{2,1,0:T(8,128)(2,1)S(1)} %broadcast_in_dim.27), channel_id=1, replica_groups=mesh['y'=8,'x'=4,'z'=8,'c'=2] {'y','x'}, dimensions={0} | all-to-all | bytes 524288 | tf_op jit(solution)/shard_map/readout/all_to_all | solution.py:225
  175.9 1.8 place.1
  (34 shorter events, 0.2 us)
Async XLA Ops:
  6.5 11.8 %copy-start.3 = (bf16[1024,128]{1,0:T(8,128)(2,1)S(1)}, bf16[1024,128]{1,0:T(8,128)(2,1)}, u32[]{:S(2)}) copy-start(bf16[1024,128]{1,0:T(8,128)(2,1)} %param.8) | copy-start | bytes 786436
  6.5 13.9 %copy-start.4 = (bf16[2048,64]{0,1:T(8,128)(2,1)S(1)}, bf16[2048,64]{0,1:T(8,128)(2,1)}, u32[]{:S(2)}) copy-start(bf16[2048,64]{0,1:T(8,128)(2,1)} %param.9) | copy-start | bytes 786436
  6.5 16.3 %copy-start = (bf16[768,1024]{1,0:T(8,128)(2,1)S(1)}, bf16[768,1024]{1,0:T(8,128)(2,1)}, u32[]{:S(2)}) copy-start(bf16[768,1024]{1,0:T(8,128)(2,1)} %param.6) | copy-start | bytes 4718596
  6.5 16.3 %copy-start.9 = (f32[1024]{0:T(1024)S(1)}, f32[1024]{0:T(1024)}, u32[]{:S(2)}) copy-start(f32[1024]{0:T(1024)} %param.7) | copy-start | bytes 12292
  6.5 89.3 %all-gather.2.cloned.1.call-start = ((), (), s32[]{:S(2)}) async-start(), calls=%async_computation.2 | async-start | bytes 3538944 | tf_op jit(solution)/shard_map/all_gather | solution.py:250
  9.5 15.4 %copy-start.6 = (bf16[128,768]{1,0:T(8,128)(2,1)}, bf16[128,768]{1,0:T(8,128)(2,1)S(1)}, u32[]{:S(2)}) copy-start(bf16[128,768]{1,0:T(8,128)(2,1)S(1)} %slice.59.refs_0_) | copy-start | bytes 589828
  9.5 42.8 %collective-permute-start.2 = (bf16[128,768]{1,0:T(8,128)(2,1)S(1)}, bf16[128,768]{1,0:T(8,128)(2,1)S(1)}, u32[]{:S(2)}, u32[]{:S(2)}) collective-permute-start(bf16[128,768]{1,0:T(8,128)(2,1)S(1)} %slice.59.refs_0_), channel_id=1, source_target_pairs={{0,2},{2,4},{4,6},{6,8},{8,10},{10,12},{12,14},{14,0},{1,3},{3,5},... | collective-permute-start | bytes 589832 | tf_op jit(solution)/shard_map/ppermute | solution.py:234
  13.8 42.7 %collective-permute-start.3 = (bf16[128,768]{1,0:T(8,128)(2,1)S(1)}, bf16[128,768]{1,0:T(8,128)(2,1)S(1)}, u32[]{:S(2)}, u32[]{:S(2)}) collective-permute-start(bf16[128,768]{1,0:T(8,128)(2,1)S(1)} %slice.59.refs_0_), channel_id=1, source_target_pairs={{0,14},{2,0},{4,2},{6,4},{8,6},{10,8},{12,10},{14,12},{1,15},{3,1}... | collective-permute-start | bytes 589832 | tf_op jit(solution)/shard_map/ppermute | solution.py:234
  18.5 39.9 %collective-permute-start = (bf16[1024,128]{0,1:T(8,128)(2,1)S(1)}, bf16[1024,128]{0,1:T(8,128)(2,1)S(1)}, u32[]{:S(2)}, u32[]{:S(2)}) collective-permute-start(bf16[1024,128]{0,1:T(8,128)(2,1)S(1)} %copy.21), channel_id=1, source_target_pairs={{0,1},{1,0},{2,3},{3,2},{4,5},{5,4},{6,7},{7,6},{8,9},{9,8},{10,11... | collective-permute-start | bytes 786440 | tf_op jit(solution)/shard_map/ppermute | solution.py:234
  20.5 38.0 %collective-permute-start.1 = (bf16[64,2048]{1,0:T(8,128)(2,1)S(1)}, bf16[64,2048]{1,0:T(8,128)(2,1)S(1)}, u32[]{:S(2)}, u32[]{:S(2)}) collective-permute-start(bf16[64,2048]{1,0:T(8,128)(2,1)S(1)} %bitcast.57), channel_id=1, source_target_pairs={{0,1},{1,0},{2,3},{3,2},{4,5},{5,4},{6,7},{7,6},{8,9},{9,8},{10,11... | collective-permute-start | bytes 786440 | tf_op jit(solution)/shard_map/ppermute | solution.py:234
  52.3 9.4 %copy-start.11 = (bf16[128,768]{1,0:T(8,128)(2,1)}, bf16[128,768]{1,0:T(8,128)(2,1)S(1)}, u32[]{:S(2)}) copy-start(bf16[128,768]{1,0:T(8,128)(2,1)S(1)} %collective-permute-done.2.refs_1_) | copy-start | bytes 589828
  52.3 12.1 %collective-permute-start.4 = (bf16[128,768]{1,0:T(8,128)(2,1)S(1)}, bf16[128,768]{1,0:T(8,128)(2,1)S(1)}, u32[]{:S(2)}, u32[]{:S(2)}) collective-permute-start(bf16[128,768]{1,0:T(8,128)(2,1)S(1)} %collective-permute-done.2.refs_1_), channel_id=1, source_target_pairs={{0,2},{2,4},{4,6},{6,8},{8,10},{10,12},{12,14},{14,0},{1,3},{3,5},... | collective-permute-start | bytes 589832 | tf_op jit(solution)/shard_map/ppermute | solution.py:234
  56.5 5.2 %copy-start.12 = (bf16[128,768]{1,0:T(8,128)(2,1)}, bf16[128,768]{1,0:T(8,128)(2,1)S(1)}, u32[]{:S(2)}) copy-start(bf16[128,768]{1,0:T(8,128)(2,1)S(1)} %collective-permute-done.3.refs_2_) | copy-start | bytes 589828
  56.5 10.2 %collective-permute-start.5 = (bf16[128,768]{1,0:T(8,128)(2,1)S(1)}, bf16[128,768]{1,0:T(8,128)(2,1)S(1)}, u32[]{:S(2)}, u32[]{:S(2)}) collective-permute-start(bf16[128,768]{1,0:T(8,128)(2,1)S(1)} %collective-permute-done.3.refs_2_), channel_id=1, source_target_pairs={{0,14},{2,0},{4,2},{6,4},{8,6},{10,8},{12,10},{14,12},{1,15},{3,1}... | collective-permute-start | bytes 589832 | tf_op jit(solution)/shard_map/ppermute | solution.py:234
  58.5 3.2 %copy-start.5 = (bf16[64,2048]{1,0:T(8,128)(2,1)}, bf16[64,2048]{1,0:T(8,128)(2,1)S(1)}, u32[]{:S(2)}) copy-start(bf16[64,2048]{1,0:T(8,128)(2,1)S(1)} %collective-permute-done.1) | copy-start | bytes 786436
  61.8 34.0 %copy-start.1 = (bf16[768,128]{1,0:T(8,128)(2,1)}, bf16[768,128]{1,0:T(8,128)(2,1)S(1)}, u32[]{:S(2)}) copy-start(bf16[768,128]{1,0:T(8,128)(2,1)S(1)} %get-tuple-element.14.refs_2_) | copy-start | bytes 589828
  61.8 34.0 %copy-start.2 = (bf16[768,128]{1,0:T(8,128)(2,1)}, bf16[768,128]{1,0:T(8,128)(2,1)S(1)}, u32[]{:S(2)}) copy-start(bf16[768,128]{1,0:T(8,128)(2,1)S(1)} %get-tuple-element.13.refs_2_) | copy-start | bytes 589828
  61.8 19.9 %copy-start.10 = (f32[2,128]{1,0:T(2,128)}, f32[2,128]{1,0:T(2,128)S(1)}, u32[]{:S(2)}) copy-start(f32[2,128]{1,0:T(2,128)S(1)} %broadcast_multiply_fusion.2) | copy-start | bytes 3076
  64.4 17.2 %copy-start.13 = (bf16[128,768]{1,0:T(8,128)(2,1)}, bf16[128,768]{1,0:T(8,128)(2,1)S(1)}, u32[]{:S(2)}) copy-start(bf16[128,768]{1,0:T(8,128)(2,1)S(1)} %collective-permute-done.4.refs_3_) | copy-start | bytes 589828
  64.4 7.6 %collective-permute-start.6 = (bf16[128,768]{1,0:T(8,128)(2,1)S(1)}, bf16[128,768]{1,0:T(8,128)(2,1)S(1)}, u32[]{:S(2)}, u32[]{:S(2)}) collective-permute-start(bf16[128,768]{1,0:T(8,128)(2,1)S(1)} %collective-permute-done.4.refs_3_), channel_id=1, source_target_pairs={{0,2},{2,4},{4,6},{6,8},{8,10},{10,12},{12,14},{14,0},{1,3},{3,5},... | collective-permute-start | bytes 589832 | tf_op jit(solution)/shard_map/ppermute | solution.py:234
  66.7 15.0 %copy-start.14 = (bf16[128,768]{1,0:T(8,128)(2,1)}, bf16[128,768]{1,0:T(8,128)(2,1)S(1)}, u32[]{:S(2)}) copy-start(bf16[128,768]{1,0:T(8,128)(2,1)S(1)} %collective-permute-done.5.refs_4_) | copy-start | bytes 589828
  66.7 7.6 %collective-permute-start.7 = (bf16[128,768]{1,0:T(8,128)(2,1)S(1)}, bf16[128,768]{1,0:T(8,128)(2,1)S(1)}, u32[]{:S(2)}, u32[]{:S(2)}) collective-permute-start(bf16[128,768]{1,0:T(8,128)(2,1)S(1)} %collective-permute-done.5.refs_4_), channel_id=1, source_target_pairs={{0,14},{2,0},{4,2},{6,4},{8,6},{10,8},{12,10},{14,12},{1,15},{3,1}... | collective-permute-start | bytes 589832 | tf_op jit(solution)/shard_map/ppermute | solution.py:234
  72.0 9.7 %copy-start.7 = (bf16[128,768]{1,0:T(8,128)(2,1)}, bf16[128,768]{1,0:T(8,128)(2,1)S(1)}, u32[]{:S(2)}) copy-start(bf16[128,768]{1,0:T(8,128)(2,1)S(1)} %collective-permute-done.6.refs_5_) | copy-start | bytes 589828
  72.0 7.6 %collective-permute-start.8 = (bf16[64,768]{1,0:T(8,128)(2,1)S(1)}, bf16[64,768]{1,0:T(8,128)(2,1)S(1)}, u32[]{:S(2)}, u32[]{:S(2)}) collective-permute-start(bf16[64,768]{1,0:T(8,128)(2,1)S(1)} %slice.74), channel_id=1, source_target_pairs={{0,2},{2,4},{4,6},{6,8},{8,10},{10,12},{12,14},{14,0},{1,3},{3,5},... | collective-permute-start | bytes 294920 | tf_op jit(solution)/shard_map/ppermute | solution.py:234
  74.3 7.4 %copy-start.8 = (bf16[128,768]{1,0:T(8,128)(2,1)}, bf16[128,768]{1,0:T(8,128)(2,1)S(1)}, u32[]{:S(2)}) copy-start(bf16[128,768]{1,0:T(8,128)(2,1)S(1)} %collective-permute-done.7.refs_6_) | copy-start | bytes 589828
  74.3 6.6 %collective-permute-start.9 = (bf16[64,768]{1,0:T(8,128)(2,1)S(1)}, bf16[64,768]{1,0:T(8,128)(2,1)S(1)}, u32[]{:S(2)}, u32[]{:S(2)}) collective-permute-start(bf16[64,768]{1,0:T(8,128)(2,1)S(1)} %slice.75), channel_id=1, source_target_pairs={{0,14},{2,0},{4,2},{6,4},{8,6},{10,8},{12,10},{14,12},{1,15},{3,1}... | collective-permute-start | bytes 294920 | tf_op jit(solution)/shard_map/ppermute | solution.py:234
  110.5 16.8 %collective-permute-start.10 = (bf16[32,48,128]{2,1,0:T(8,128)(2,1)}, bf16[32,48,128]{2,1,0:T(8,128)(2,1)S(1)}, u32[]{:S(2)}, u32[]{:S(2)}) collective-permute-start(bf16[32,48,128]{2,1,0:T(8,128)(2,1)} %attend.4), channel_id=1, source_target_pairs={{0,1},{1,0},{2,3},{3,2},{4,5},{5,4},{6,7},{7,6},{8,9},{9,8},{10,11... | collective-permute-start | bytes 1179656 | tf_op jit(solution)/shard_map/totals/ppermute | solution.py:234
Sparse Core Ops, SparseCore 0:
  9.5 55.6 all-gather.1

commit v3 on v2

--- a/solution.py
+++ b/solution.py
@@ -24,39 +24,61 @@
     return high, (value - high.astype(F32)).astype(BF16)
 
 
-def attend_kernel(pieces, heads, first, last, *refs):
-    xs, refs = refs[:pieces], refs[pieces:]
-    rstd_ref, w_ref, b_ref, q_ref = refs[:4]
-    refs = refs[4:]
-    if not first:
+def attend_kernel(mode, pieces, *refs):
+    if mode != "end":
+        xs, (rstd_ref, w_ref, b_ref), refs = refs[:pieces], refs[pieces : pieces + 3], refs[pieces + 3 :]
+    else:
+        (k_ref, v_ref), refs = refs[:2], refs[2:]
+    q_ref, refs = refs[0], refs[1:]
+    heads, size, latents = q_ref.shape
+    if mode != "first":
         acc_ins, m_ins, refs = refs[:heads], refs[heads : 2 * heads], refs[2 * heads :]
-    if last:
         pay_ref, refs = refs[0], refs[1:]
+    if mode == "mid":
+        (k_out, v_out), refs = refs[:2], refs[2:]
     acc_refs, m_refs, refs = refs[:heads], refs[heads : 2 * heads], refs[2 * heads :]
-    k_ref, v_ref, qa_ref = refs
+    qa_ref, refs = refs[0], refs[1:]
+    if mode != "end":
+        (k_ref, v_ref), refs = refs[:2], refs[2:]
     tokens = k_ref.shape[1]
-    _, size, latents = q_ref.shape
     block = min(BLOCK, tokens)
     steps = tokens // block
+    keys_of = [k_ref.at[0], k_out.at[0]] if mode == "mid" else [k_ref.at[h] for h in range(heads)]
+    values_of = [v_ref.at[0], v_out.at[0]] if mode == "mid" else [v_ref.at[h] for h in range(heads)]
 
     def project(x, start, count):
         kv = jnp.dot(x, w_ref[...], preferred_element_type=F32)
         kv = (kv + b_ref[...]) * rstd_ref[pl.ds(start, count), :]
         lane = lax.broadcasted_iota(jnp.int32, (count, 2 * size), 1)
-        for h in range(heads):
+        for h in range(2):
             mine = kv[:, 2 * size * h : 2 * size * (h + 1)]
-            k_ref[h, pl.ds(start, count), :] = jnp.where(lane < size, mine, 1.0).astype(BF16)
-            v_ref[h, :size, pl.ds(start, count)] = mine.T[size:, :].astype(BF16)
-
-    start = 0
-    for x_ref in xs:
-        count = min(512, x_ref.shape[0])
-        for t in range(x_ref.shape[0] // count):
-            project(x_ref[pl.ds(t * count, count), :], start, count)
+            keys_of[h][pl.ds(start, count), :] = jnp.where(lane < size, mine, 1.0).astype(BF16)
+            values_of[h][:size, pl.ds(start, count)] = mine.T[size:, :].astype(BF16)
+
+    if mode == "first":
+        start = 0
+        for x_ref in xs:
+            count = x_ref.shape[0]
+            project(x_ref[...], start, count)
             start += count
+    if mode == "mid":
+        x_buf, sems = refs
+        count = tokens // 4
+        copies = [
+            pltpu.make_async_copy(xs[0].at[pl.ds(t * count, count)], x_buf.at[t], sems.at[t])
+            for t in range(4)
+        ]
+        for copy in copies:
+            copy.start()
+        for t in range(4):
+            copies[t].wait()
+            project(x_buf[t], t * count, count)
+    if mode != "end":
+        for h in range(2):
+            values_of[h][size:, :] = jnp.ones((ROWS - size, tokens), BF16)
 
     def scores(h, keys):
-        return lax.dot_general(k_ref[h, keys, :], qa_ref[h], PLAIN, preferred_element_type=F32)
+        return lax.dot_general(keys_of[h][keys, :], qa_ref[h], PLAIN, preferred_element_type=F32)
 
     def set_max(h, value):
         high, low = split(value)
@@ -66,23 +88,25 @@
         )
 
     for h in range(heads):
-        v_ref[h, size:, :] = jnp.ones((ROWS - size, tokens), BF16)
         qa_ref[h, :size, :] = q_ref[h]
         qa_ref[h, size:, :] = jnp.zeros((size, latents), BF16)
-        if first:
+        if mode == "first":
             set_max(h, jnp.max(scores(h, pl.ds(0, 128)), axis=0, keepdims=True))
         else:
             set_max(h, m_ins[h][...])
 
     def add(h, keys):
         probs = jnp.exp2(scores(h, keys)).astype(BF16)
-        acc_refs[h][...] += lax.dot_general(v_ref[h, :, keys], probs, PLAIN, preferred_element_type=F32)
+        return lax.dot_general(values_of[h][:, keys], probs, PLAIN, preferred_element_type=F32)
 
     for h in range(heads):
         acc_ref, m_ref = acc_refs[h], m_refs[h]
-        acc_ref[...] = jnp.zeros((ROWS, latents), F32) if first else acc_ins[h][...]
         for t in range(steps):
-            add(h, pl.ds(t * block, block))
+            more = add(h, pl.ds(t * block, block))
+            if t > 0:
+                acc_ref[...] += more
+            else:
+                acc_ref[...] = more if mode == "first" else acc_ins[h][...] + more
 
         @pl.when(jnp.logical_not(jnp.max(acc_ref[size : size + 8, :]) < LIMIT))
         def _(h=h, acc_ref=acc_ref, m_ref=m_ref):
@@ -96,18 +120,18 @@
                 return jnp.maximum(best, jnp.max(scores(h, at(t)), axis=0, keepdims=True))
 
             set_max(h, lax.fori_loop(0, steps, widen, before))
-            if first:
+            if mode == "first":
                 acc_ref[...] = jnp.zeros((ROWS, latents), F32)
             else:
                 acc_ref[...] = acc_ins[h][...] * jnp.exp2(before - m_ref[...])
 
             def redo(t, carry):
-                add(h, at(t))
+                acc_ref[...] += add(h, at(t))
                 return carry
 
             lax.fori_loop(0, steps, redo, 0)
 
-        if last:
+        if mode != "first":
             for i in range(latents // 128):
                 lanes = pl.ds(128 * i, 128)
                 acc, total, m = acc_ref[:size, lanes], acc_ref[size : size + 1, lanes], m_ref[:, lanes]
@@ -139,63 +163,90 @@
     return jnp.concatenate(rows, axis=0).astype(BF16)
 
 
-def attend(xs, rstd, w, b, q, state, last):
+def attend(mode, source, q, state=()):
     heads, size, latents = q.shape
-    tokens = sum(x.shape[0] for x in xs)
-    first = state is None
     vmem = pl.BlockSpec(memory_space=pltpu.VMEM)
+    pieces = len(source) - 3
+    tokens = source[0].shape[1] if mode == "end" else sum(x.shape[0] for x in source[:pieces])
     accs = [jax.ShapeDtypeStruct((ROWS, latents), F32)] * heads
     ms = [jax.ShapeDtypeStruct((1, latents), F32)] * heads
-    scratch = [
-        pltpu.VMEM((heads, tokens, 2 * size), BF16),
-        pltpu.VMEM((heads, ROWS, tokens), BF16),
-        pltpu.VMEM((heads, 2 * size, latents), BF16),
-    ]
-    if last:
-        out = jax.ShapeDtypeStruct((latents // 64, PAY, 128), BF16)
+    keys = jax.ShapeDtypeStruct((heads, tokens, 2 * size), BF16)
+    values = jax.ShapeDtypeStruct((heads, ROWS, tokens), BF16)
+    pay = jax.ShapeDtypeStruct((latents // 64, PAY, 128), BF16)
+    ins = (*source, q, *state)
+    in_specs = [vmem] * len(ins)
+    scratch = [pltpu.VMEM((heads, 2 * size, latents), BF16)]
+    if mode != "end":
+        scratch += [pltpu.VMEM(keys.shape, BF16), pltpu.VMEM(values.shape, BF16)]
+    out = accs + ms
+    if mode != "first":
         scratch = [pltpu.VMEM(i.shape, F32) for i in accs + ms] + scratch
-    else:
-        out = accs + ms
-    ins = (*xs, rstd, w, b, q) + (() if first else tuple(state))
+        out = [pay]
+    if mode == "mid":
+        out = [pay, keys, values]
+        in_specs[0] = pl.BlockSpec(memory_space=pl.ANY)
+        scratch += [
+            pltpu.VMEM((4, tokens // 4, source[0].shape[1]), BF16),
+            pltpu.SemaphoreType.DMA((4,)),
+        ]
     work = tokens * latents * heads
     return pl.pallas_call(
-        functools.partial(attend_kernel, len(xs), heads, first, last),
+        functools.partial(attend_kernel, mode, pieces),
         out_shape=out,
-        in_specs=[vmem] * len(ins),
-        out_specs=jax.tree.map(lambda _: vmem, out),
+        in_specs=in_specs,
+        out_specs=[vmem] * len(out),
         scratch_shapes=scratch,
         compiler_params=pltpu.CompilerParams(vmem_limit_bytes=56 << 20),
         cost_estimate=pl.CostEstimate(
-            flops=16 * work * size, bytes_accessed=tokens * w.shape[0] * 2, transcendentals=work
+            flops=16 * work * size, bytes_accessed=tokens * 1536, transcendentals=work
         ),
         name="attend",
     )(*ins)
 
 
-def combine_kernel(final, parts_ref, out_ref):
-    count, blocks = parts_ref.shape[:2]
+def merge(parts):
     half = 32
-    for j in range(blocks):
-        parts = [parts_ref[i, j].astype(F32) for i in range(count)]
-        ms = [p[half + 2 : half + 3] + p[half + 3 : half + 4] for p in parts]
-        top = functools.reduce(jnp.maximum, ms)
-        acc, total = 0.0, 0.0
-        for p, m in zip(parts, ms):
-            factor = jnp.exp2(m - top)
-            acc = acc + p[:half] * factor
-            total = total + (p[half : half + 1] + p[half + 1 : half + 2]) * factor
-        out_ref[j] = (acc / total).astype(BF16) if final else pack(acc, total, top)
-
-
-def combine(parts, final=False):
+    ms = [p[half + 2 : half + 3] + p[half + 3 : half + 4] for p in parts]
+    top = functools.reduce(jnp.maximum, ms)
+    acc, total = 0.0, 0.0
+    for p, m in zip(parts, ms):
+        factor = jnp.exp2(m - top)
+        acc = acc + p[:half] * factor
+        total = total + (p[half : half + 1] + p[half + 1 : half + 2]) * factor
+    return acc, total, top
+
+
+def combine_kernel(one_ref, two_ref, out_ref):
+    for j in range(one_ref.shape[0]):
+        out_ref[j] = pack(*merge([one_ref[j].astype(F32), two_ref[j].astype(F32)]))
+
+
+def finish_kernel(parts_ref, out_ref):
+    acc, total, _ = merge([parts_ref[i].astype(F32) for i in range(parts_ref.shape[0])])
+    result = (acc / total).astype(BF16)
+    for i in range(out_ref.shape[0]):
+        out_ref[i] = result
+
+
+def combine(one, two):
     vmem = pl.BlockSpec(memory_space=pltpu.VMEM)
-    rows = 32 if final else PAY
     return pl.pallas_call(
-        functools.partial(combine_kernel, final),
-        out_shape=jax.ShapeDtypeStruct((parts.shape[1], rows, 128), BF16),
+        combine_kernel,
+        out_shape=jax.ShapeDtypeStruct(one.shape, BF16),
+        in_specs=[vmem] * 2,
+        out_specs=vmem,
+        name="combine",
+    )(one, two)
+
+
+def finish(parts):
+    vmem = pl.BlockSpec(memory_space=pltpu.VMEM)
+    return pl.pallas_call(
+        finish_kernel,
+        out_shape=jax.ShapeDtypeStruct((parts.shape[0], 32, 128), BF16),
         in_specs=[vmem],
         out_specs=vmem,
-        name="combine",
+        name="finish",
     )(parts)
 
 
@@ -225,10 +276,6 @@
     return lax.all_to_all(parts, axis, split_axis=0, concat_axis=0, tiled=True)
 
 
-def spread(block, axis):
-    return exchange(jnp.broadcast_to(block[None], (lax.axis_size(axis[0]) * lax.axis_size(axis[1]),) + block.shape), axis)
-
-
 def shift(block, axis, by):
     size = lax.axis_size(axis)
     return lax.ppermute(block, axis, [(i, (i + by) % size) for i in range(size)])
@@ -257,8 +304,7 @@
     mean = jnp.mean(embed, axis=-1, keepdims=True)
     var = jnp.mean((embed - mean) * (embed - mean), axis=-1)
     rstd = lax.rsqrt(var + 1e-05)
-    rstd = lax.all_gather(rstd.reshape(tokens // 128, 128), "z", axis=0, tiled=False)
-    rstd = rstd.reshape(-1, tokens)
+    rstd = exchange(jnp.broadcast_to(rstd[None], (lax.axis_size("z"), tokens)), "z")
     turned = jnp.concatenate([rstd, rstd])[:, :RING]
     turned = lax.dynamic_slice_in_dim(turned, lax.axis_index("z"), 8, axis=0)
     order = [0, 7, 1, 6, 2, 5, 3, 4]
@@ -273,23 +319,18 @@
     fold_bias = jnp.einsum("d,hdn->hn", bias, w_pair.astype(F32), precision=lax.Precision.HIGHEST)
     fold_bias = fold_bias * scale
 
-    state = attend(
-        blocks, rstd_ring, jnp.concatenate([fold[0], fold[1]], axis=1),
-        fold_bias.reshape(1, -1), q_pair, None, False,
+    both_heads = (jnp.concatenate([fold[0], fold[1]], axis=1), fold_bias.reshape(1, -1))
+    state = attend("first", (*blocks, rstd_ring, *both_heads), q_pair)
+    other, keys, values = attend(
+        "mid", (rest, rstd_rest, *both_heads), q_pair[:1], (state[0], state[2])
     )
-    pays = [
-        attend(
-            [rest], rstd_rest, fold[h], fold_bias[h][None], q_pair[h : h + 1],
-            (state[h], state[2 + h]), True,
-        )
-        for h in range(2)
-    ]
+    arrived = shift(other, "c", 1)
+    (own,) = attend("end", (keys, values), q_pair[1:], (state[1], state[3]))
 
     with jax.named_scope("totals"):
-        part = combine(jnp.stack([shift(pays[0], "c", 1), pays[1]]))
-        out = combine(exchange(part[:, None], ("y", "x")), final=True)
+        part = finish(exchange(combine(own, arrived), ("y", "x")))
     with jax.named_scope("readout"):
-        return place(spread(out[0], ("y", "x"))).T
+        return place(exchange(part, ("y", "x"))).T
 
 
 def solution(mesh):

time: 185 us -> 180 us (0.973)
  the two profiles are of different devices: /device:TPU:64 before, /device:TPU:192 now
where the time goes in v3:
time: 180 us
  Pallas kernels  49.3 us (27%)
  starting transfers between devices  42.9 us (24%)
  blocking collectives  42.7 us (24%)
  waiting for transfers between devices  15.1 us (8%)
  between operations  14.3 us (8%)
  local copies, waits for them, and re-layouts  6.91 us (4%)
  other arithmetic  4.19 us (2%)
  matrix products  4.18 us (2%)
    pallas_call x3, Pallas kernels, attend(): pl.pallas_call(functools.partial(attend_kernel, mode, pieces), out_shape=...  43.6 us
    all_to_all x2, blocking collectives, exchange(): return lax.all_to_all(parts, axis, split_axis=0, concat_axis=0, tiled=True)  42.7 us
    ppermute x11, starting transfers between devices, shift(): lax.ppermute(block, axis, [(i, (i + by) % size) for i in range(size)])  35.2 us
    ppermute x11, waiting for transfers between devices, shift(): lax.ppermute(block, axis, [(i, (i + by) % size) for i in range(size)])  15 us
    all_to_all x1, starting transfers between devices, exchange(): return lax.all_to_all(parts, axis, split_axis=0, concat_axis=0, tiled=True)  7.76 us
  transfers between devices with their start and end apart: 13, of which 4 were waited for; matrix products, arithmetic and copies ran while one was open for 7% of the time, Pallas kernels for 15%

profile of v3, /device:TPU:192, one launch (start us, length us, event | category | flops | bytes accessed | tf_op | source)
XLA Modules:
  0.0 179.6 jit_solution(17272392920597537101)
XLA Ops:
  6.5 0.0 all-gather.2.cloned.1.call-start
  6.5 1.9 %slice.47 = bf16[256,768]{1,0:T(8,128)(2,1)} slice(bf16[384,768]{1,0:T(8,128)(2,1)} %param.5), slice={[128:384], [0:768]} | slice | bytes 786432 | tf_op jit(solution)/shard_map/slice | solution.py:297
  8.4 0.0 all-gather.2.cloned.1.call-update
  8.5 0.9 slice.51.refs_0_
  9.4 0.0 copy-start.5
  9.4 5.5 %collective-permute-start.2 = (bf16[128,768]{1,0:T(8,128)(2,1)S(1)}, bf16[128,768]{1,0:T(8,128)(2,1)S(1)}, u32[]{:S(2)}, u32[]{:S(2)}) collective-permute-start(bf16[128,768]{1,0:T(8,128)(2,1)S(1)} %slice.51.refs_0_), channel_id=1, source_target_pairs={{0,2},{2,4},{4,6},{6,8},{8,10},{10,12},{12,14},{14,0},{1,3},{3,5},... | collective-permute-start | bytes 589832 | tf_op jit(solution)/shard_map/ppermute | solution.py:281
  14.9 1.9 %collective-permute-start.3 = (bf16[128,768]{1,0:T(8,128)(2,1)S(1)}, bf16[128,768]{1,0:T(8,128)(2,1)S(1)}, u32[]{:S(2)}, u32[]{:S(2)}) collective-permute-start(bf16[128,768]{1,0:T(8,128)(2,1)S(1)} %slice.51.refs_0_), channel_id=1, source_target_pairs={{0,14},{2,0},{4,2},{6,4},{8,6},{10,8},{12,10},{14,12},{1,15},{3,1}... | collective-permute-start | bytes 589832 | tf_op jit(solution)/shard_map/ppermute | solution.py:281
  16.8 0.0 copy-done
  16.9 1.9 %fusion.15 = (f32[384]{0:T(512)S(1)}, f32[384,1024]{1,0:T(8,128)S(1)}) fusion(f32[1024]{0:T(1024)} %param.7, bf16[384,768]{1,0:T(8,128)(2,1)} %param.5, bf16[768,1024]{1,0:T(8,128)(2,1)S(1)} %copy-done), kind=kOutput, calls=%fused_computation.28 | convolution fusion | flops 604765824 | bytes 3741184 | tf_op jit(solution)/shard_map/dot_general | solution.py:303
  18.8 0.0 copy-start.2
  18.8 0.0 copy-start.3
  18.8 0.0 copy-start.8
  18.8 0.3 multiply_reduce_fusion
  19.1 0.6 broadcast_in_dim.8
  19.8 7.8 %all-to-all-start = ((f32[8,1,384]{2,1,0:T(1,128)}), f32[8,1,384]{2,1,0:T(1,128)S(1)}, u32[]{:S(2)}, u32[]{:S(2)}) async-start(f32[8,1,384]{2,1,0:T(1,128)} %broadcast_in_dim.8), calls=%async_computation | async-start | bytes 24576 | tf_op jit(solution)/shard_map/all_to_all | solution.py:276
  27.5 0.0 copy-done.2
  27.5 0.1 copy.14
  27.7 1.9 %collective-permute-start = (bf16[1024,128]{0,1:T(8,128)(2,1)S(1)}, bf16[1024,128]{0,1:T(8,128)(2,1)S(1)}, u32[]{:S(2)}, u32[]{:S(2)}) collective-permute-start(bf16[1024,128]{0,1:T(8,128)(2,1)S(1)} %copy.14), channel_id=1, source_target_pairs={{0,1},{1,0},{2,3},{3,2},{4,5},{5,4},{6,7},{7,6},{8,9},{9,8},{10,11... | collective-permute-start | bytes 786440 | tf_op jit(solution)/shard_map/ppermute | solution.py:281
  29.6 0.0 copy-done.3
  29.6 2.4 %collective-permute-start.1 = (bf16[64,2048]{1,0:T(8,128)(2,1)S(1)}, bf16[64,2048]{1,0:T(8,128)(2,1)S(1)}, u32[]{:S(2)}, u32[]{:S(2)}) collective-permute-start(bf16[64,2048]{1,0:T(8,128)(2,1)S(1)} %bitcast.46), channel_id=1, source_target_pairs={{0,1},{1,0},{2,3},{3,2},{4,5},{5,4},{6,7},{7,6},{8,9},{9,8},{10,11... | collective-permute-start | bytes 786440 | tf_op jit(solution)/shard_map/ppermute | solution.py:281
  32.0 0.6 reduce_sum.39
  33.2 0.3 convert_reduce_fusion
  33.5 0.0 all-to-all-done
  33.6 1.0 copy.17.refs_8_
  34.6 1.4 copy.22
  36.0 0.0 collective-permute-done.2.refs_1_
  36.0 4.6 %collective-permute-start.4 = (bf16[128,768]{1,0:T(8,128)(2,1)S(1)}, bf16[128,768]{1,0:T(8,128)(2,1)S(1)}, u32[]{:S(2)}, u32[]{:S(2)}) collective-permute-start(bf16[128,768]{1,0:T(8,128)(2,1)S(1)} %collective-permute-done.2.refs_1_), channel_id=1, source_target_pairs={{0,2},{2,4},{4,6},{6,8},{8,10},{10,12},{12,14},{14,0},{1,3},{3,5},... | collective-permute-start | bytes 589832 | tf_op jit(solution)/shard_map/ppermute | solution.py:281
  40.6 0.0 collective-permute-done.3.refs_2_
  40.6 1.9 %collective-permute-start.5 = (bf16[128,768]{1,0:T(8,128)(2,1)S(1)}, bf16[128,768]{1,0:T(8,128)(2,1)S(1)}, u32[]{:S(2)}, u32[]{:S(2)}) collective-permute-start(bf16[128,768]{1,0:T(8,128)(2,1)S(1)} %collective-permute-done.3.refs_2_), channel_id=1, source_target_pairs={{0,14},{2,0},{4,2},{6,4},{8,6},{10,8},{12,10},{14,12},{1,15},{3,1}... | collective-permute-start | bytes 589832 | tf_op jit(solution)/shard_map/ppermute | solution.py:281
  42.5 0.0 collective-permute-done
  42.5 0.1 pad_maximum_fusion
  42.6 1.8 fusion.10
  44.4 0.5 fusion.16
  44.9 0.0 collective-permute-done.1
  44.9 0.0 copy-start.4
  44.9 0.9 pad_maximum_fusion.1.refs_11_
  45.8 3.6 %collective-permute-done.4.refs_3_ = bf16[128,768]{1,0:T(8,128)(2,1)S(1)} collective-permute-done((bf16[128,768]{1,0:T(8,128)(2,1)S(1)}, bf16[128,768]{1,0:T(8,128)(2,1)S(1)}, u32[]{:S(2)}, u32[]{:S(2)}) %collective-permute-start.4) | collective-permute-done | bytes 196640 | tf_op jit(solution)/shard_map/ppermute | solution.py:281
  49.5 5.6 %collective-permute-start.6 = (bf16[128,768]{1,0:T(8,128)(2,1)S(1)}, bf16[128,768]{1,0:T(8,128)(2,1)S(1)}, u32[]{:S(2)}, u32[]{:S(2)}) collective-permute-start(bf16[128,768]{1,0:T(8,128)(2,1)S(1)} %collective-permute-done.4.refs_3_), channel_id=1, source_target_pairs={{0,2},{2,4},{4,6},{6,8},{8,10},{10,12},{12,14},{14,0},{1,3},{3,5},... | collective-permute-start | bytes 589832 | tf_op jit(solution)/shard_map/ppermute | solution.py:281
  55.1 0.1 collective-permute-done.5.refs_4_
  55.2 1.9 %collective-permute-start.7 = (bf16[128,768]{1,0:T(8,128)(2,1)S(1)}, bf16[128,768]{1,0:T(8,128)(2,1)S(1)}, u32[]{:S(2)}, u32[]{:S(2)}) collective-permute-start(bf16[128,768]{1,0:T(8,128)(2,1)S(1)} %collective-permute-done.5.refs_4_), channel_id=1, source_target_pairs={{0,14},{2,0},{4,2},{6,4},{8,6},{10,8},{12,10},{14,12},{1,15},{3,1}... | collective-permute-start | bytes 589832 | tf_op jit(solution)/shard_map/ppermute | solution.py:281
  57.1 0.5 broadcast_multiply_fusion.2
  57.7 6.2 %collective-permute-done.6.refs_5_ = bf16[128,768]{1,0:T(8,128)(2,1)S(1)} collective-permute-done((bf16[128,768]{1,0:T(8,128)(2,1)S(1)}, bf16[128,768]{1,0:T(8,128)(2,1)S(1)}, u32[]{:S(2)}, u32[]{:S(2)}) %collective-permute-start.6) | collective-permute-done | bytes 196640 | tf_op jit(solution)/shard_map/ppermute | solution.py:281
  63.9 5.6 %collective-permute-start.8 = (bf16[64,768]{1,0:T(8,128)(2,1)S(1)}, bf16[64,768]{1,0:T(8,128)(2,1)S(1)}, u32[]{:S(2)}, u32[]{:S(2)}) collective-permute-start(bf16[64,768]{1,0:T(8,128)(2,1)S(1)} %slice.65), channel_id=1, source_target_pairs={{0,2},{2,4},{4,6},{6,8},{8,10},{10,12},{12,14},{14,0},{1,3},{3,5},... | collective-permute-start | bytes 294920 | tf_op jit(solution)/shard_map/ppermute | solution.py:281
  69.5 0.0 collective-permute-done.7.refs_6_
  69.6 1.9 %collective-permute-start.9 = (bf16[64,768]{1,0:T(8,128)(2,1)S(1)}, bf16[64,768]{1,0:T(8,128)(2,1)S(1)}, u32[]{:S(2)}, u32[]{:S(2)}) collective-permute-start(bf16[64,768]{1,0:T(8,128)(2,1)S(1)} %slice.66), channel_id=1, source_target_pairs={{0,14},{2,0},{4,2},{6,4},{8,6},{10,8},{12,10},{14,12},{1,15},{3,1}... | collective-permute-start | bytes 294920 | tf_op jit(solution)/shard_map/ppermute | solution.py:281
  71.5 0.8 pad_maximum_fusion.2.refs_9_.refs_2_
  72.3 0.0 collective-permute-done.8
  72.3 5.0 %collective-permute-done.9 = bf16[64,768]{1,0:T(8,128)(2,1)S(1)} collective-permute-done((bf16[64,768]{1,0:T(8,128)(2,1)S(1)}, bf16[64,768]{1,0:T(8,128)(2,1)S(1)}, u32[]{:S(2)}, u32[]{:S(2)}) %collective-permute-start.9) | collective-permute-done | bytes 98336 | tf_op jit(solution)/shard_map/ppermute | solution.py:281
  77.3 0.7 pad_maximum_fusion.3.refs_7_
  78.0 0.0 copy-done.12
  78.0 0.0 copy-done.7
  78.0 14.1 %attend.3 = (f32[80,2048]{1,0:T(8,128)}, f32[80,2048]{1,0:T(8,128)}, f32[1,2048]{1,0:T(1,128)}, f32[1,2048]{1,0:T(1,128)}) custom-call(bf16[128,768]{1,0:T(8,128)(2,1)} %copy-done.5, bf16[128,768]{1,0:T(8,128)(2,1)} %copy-done.9, bf16[128,768]{1,0:T(8,128)(2,1)} %copy-done.10, bf16[128,768]{1,0:T(8,128)(2,1)} %copy-done.11, bf16[128,768]{1,0:T(8,128)(2,1)} %copy-done.12, ...), custom_call_target="tpu_custom_call" | custom-call | flops 4294967296 | bytes 1572864 | tf_op jit(solution)/shard_map/attend/pallas_call | solution.py:193
  92.1 0.0 copy-done.4
  92.1 0.0 all-gather.2.cloned.1.call-done.refs_0_
  92.1 16.8 %attend.4 = (bf16[32,48,128]{2,1,0:T(8,128)(2,1)}, bf16[1,2048,128]{2,1,0:T(8,128)(2,1)}, bf16[1,80,2048]{2,1,0:T(8,128)(2,1)}) custom-call(bf16[2048,768]{1,0:T(8,128)(2,1)} %all-gather.2.cloned.1.call-done.refs_0_, f32[2048,1]{1,0:T(8,128)} %bitcast.42, bf16[768,256]{1,0:T(8,128)(2,1)} %pad_maximum_fusion.2.refs_9_.refs_2_, f32[1,256]{1,0:T(1,128)} %bitcast.59, ...), custom_call_target="tpu_custom_call" | custom-call | flops 4294967296 | bytes 3145728 | tf_op jit(solution)/shard_map/attend/pallas_call | solution.py:193
  108.9 1.9 %collective-permute-start.10 = (bf16[32,48,128]{2,1,0:T(8,128)(2,1)}, bf16[32,48,128]{2,1,0:T(8,128)(2,1)S(1)}, u32[]{:S(2)}, u32[]{:S(2)}) collective-permute-start(bf16[32,48,128]{2,1,0:T(8,128)(2,1)} %get-tuple-element.18), channel_id=1, source_target_pairs={{0,1},{1,0},{2,3},{3,2},{4,5},{5,4},{6,7},{7,6},{8,9},{9,8},{10,11... | collective-permute-start | bytes 1179656 | tf_op jit(solution)/shard_map/ppermute | solution.py:281
  110.9 12.7 %attend.5.one_ref = bf16[32,48,128]{2,1,0:T(8,128)(2,1)} custom-call(bf16[1,2048,128]{2,1,0:T(8,128)(2,1)} %get-tuple-element.14.refs_0_, bf16[1,80,2048]{2,1,0:T(8,128)(2,1)} %get-tuple-element.15.refs_1_, bf16[1,64,2048]{2,1,0:T(8,128)(2,1)} %bitcast.45, f32[80,2048]{1,0:T(8,128)} %get-tuple-element.16.refs_3_, f32[1,2048]{1,0:T(1,128)} %get-tuple-element.17.refs_4_), custom_call_target="tpu_custom_call" | custom-call | flops 4294967296 | bytes 3145728 | tf_op jit(solution)/shard_map/attend/pallas_call | solution.py:193
  123.6 0.0 collective-permute-done.10.two_ref
  123.6 0.7 copy-done.1
  124.3 2.1 %combine.1 = bf16[32,48,128]{2,1,0:T(8,128)(2,1)} custom-call(bf16[32,48,128]{2,1,0:T(8,128)(2,1)} %attend.5.one_ref, bf16[32,48,128]{2,1,0:T(8,128)(2,1)} %copy-done.1), custom_call_target="tpu_custom_call" | custom-call | tf_op jit(solution)/shard_map/totals/combine/pallas_call | solution.py:233
  126.4 25.8 %all_to_all.19.parts_ref = bf16[32,48,128]{2,1,0:T(8,128)(2,1)} all-to-all(bf16[32,48,128]{2,1,0:T(8,128)(2,1)} %combine.1), channel_id=1, replica_groups=mesh['y'=8,'x'=4,'z'=8,'c'=2] {'y','x'}, dimensions={0} | all-to-all | bytes 786432 | tf_op jit(solution)/shard_map/totals/all_to_all | solution.py:276
  152.2 1.8 %finish.1 = bf16[32,32,128]{2,1,0:T(8,128)(2,1)} custom-call(bf16[32,48,128]{2,1,0:T(8,128)(2,1)} %all_to_all.19.parts_ref), custom_call_target="tpu_custom_call" | custom-call | tf_op jit(solution)/shard_map/totals/finish/pallas_call | solution.py:244
  154.0 16.9 %all_to_all.20.parts_ref = bf16[32,32,128]{2,1,0:T(8,128)(2,1)} all-to-all(bf16[32,32,128]{2,1,0:T(8,128)(2,1)} %finish.1), channel_id=1, replica_groups=mesh['y'=8,'x'=4,'z'=8,'c'=2] {'y','x'}, dimensions={0} | all-to-all | bytes 524288 | tf_op jit(solution)/shard_map/readout/all_to_all | solution.py:276
  170.9 1.8 %place.1 = bf16[64,2048]{1,0:T(8,128)(2,1)} custom-call(bf16[32,32,128]{2,1,0:T(8,128)(2,1)} %all_to_all.20.parts_ref), custom_call_target="tpu_custom_call" | custom-call | tf_op jit(solution)/shard_map/readout/place/pallas_call | solution.py:266
  (29 shorter events, 0.2 us)
Async XLA Ops:
  6.5 10.3 %copy-start = (bf16[768,1024]{1,0:T(8,128)(2,1)S(1)}, bf16[768,1024]{1,0:T(8,128)(2,1)}, u32[]{:S(2)}) copy-start(bf16[768,1024]{1,0:T(8,128)(2,1)} %param.6) | copy-start | bytes 4718596
  6.5 85.6 %all-gather.2.cloned.1.call-start = ((), (), s32[]{:S(2)}) async-start(), calls=%async_computation.3 | async-start | bytes 3538944 | tf_op jit(solution)/shard_map/all_gather | solution.py:297
  9.4 9.4 %copy-start.5 = (bf16[128,768]{1,0:T(8,128)(2,1)}, bf16[128,768]{1,0:T(8,128)(2,1)S(1)}, u32[]{:S(2)}) copy-start(bf16[128,768]{1,0:T(8,128)(2,1)S(1)} %slice.51.refs_0_) | copy-start | bytes 589828
  9.4 26.6 %collective-permute-start.2 = (bf16[128,768]{1,0:T(8,128)(2,1)S(1)}, bf16[128,768]{1,0:T(8,128)(2,1)S(1)}, u32[]{:S(2)}, u32[]{:S(2)}) collective-permute-start(bf16[128,768]{1,0:T(8,128)(2,1)S(1)} %slice.51.refs_0_), channel_id=1, source_target_pairs={{0,2},{2,4},{4,6},{6,8},{8,10},{10,12},{12,14},{14,0},{1,3},{3,5},... | collective-permute-start | bytes 589832 | tf_op jit(solution)/shard_map/ppermute | solution.py:281
  14.9 25.6 %collective-permute-start.3 = (bf16[128,768]{1,0:T(8,128)(2,1)S(1)}, bf16[128,768]{1,0:T(8,128)(2,1)S(1)}, u32[]{:S(2)}, u32[]{:S(2)}) collective-permute-start(bf16[128,768]{1,0:T(8,128)(2,1)S(1)} %slice.51.refs_0_), channel_id=1, source_target_pairs={{0,14},{2,0},{4,2},{6,4},{8,6},{10,8},{12,10},{14,12},{1,15},{3,1}... | collective-permute-start | bytes 589832 | tf_op jit(solution)/shard_map/ppermute | solution.py:281
  18.8 8.7 %copy-start.2 = (bf16[1024,128]{1,0:T(8,128)(2,1)S(1)}, bf16[1024,128]{1,0:T(8,128)(2,1)}, u32[]{:S(2)}) copy-start(bf16[1024,128]{1,0:T(8,128)(2,1)} %param.8) | copy-start | bytes 786436
  18.8 10.8 %copy-start.3 = (bf16[2048,64]{0,1:T(8,128)(2,1)S(1)}, bf16[2048,64]{0,1:T(8,128)(2,1)}, u32[]{:S(2)}) copy-start(bf16[2048,64]{0,1:T(8,128)(2,1)} %param.9) | copy-start | bytes 786436
  18.8 13.2 %copy-start.8 = (f32[1024]{0:T(1024)S(1)}, f32[1024]{0:T(1024)}, u32[]{:S(2)}) copy-start(f32[1024]{0:T(1024)} %param.7) | copy-start | bytes 12292
  19.8 13.7 %all-to-all-start = ((f32[8,1,384]{2,1,0:T(1,128)}), f32[8,1,384]{2,1,0:T(1,128)S(1)}, u32[]{:S(2)}, u32[]{:S(2)}) async-start(f32[8,1,384]{2,1,0:T(1,128)} %broadcast_in_dim.8), calls=%async_computation | async-start | bytes 24576 | tf_op jit(solution)/shard_map/all_to_all | solution.py:276
  27.7 14.8 %collective-permute-start = (bf16[1024,128]{0,1:T(8,128)(2,1)S(1)}, bf16[1024,128]{0,1:T(8,128)(2,1)S(1)}, u32[]{:S(2)}, u32[]{:S(2)}) collective-permute-start(bf16[1024,128]{0,1:T(8,128)(2,1)S(1)} %copy.14), channel_id=1, source_target_pairs={{0,1},{1,0},{2,3},{3,2},{4,5},{5,4},{6,7},{7,6},{8,9},{9,8},{10,11... | collective-permute-start | bytes 786440 | tf_op jit(solution)/shard_map/ppermute | solution.py:281
  29.6 15.3 %collective-permute-start.1 = (bf16[64,2048]{1,0:T(8,128)(2,1)S(1)}, bf16[64,2048]{1,0:T(8,128)(2,1)S(1)}, u32[]{:S(2)}, u32[]{:S(2)}) collective-permute-start(bf16[64,2048]{1,0:T(8,128)(2,1)S(1)} %bitcast.46), channel_id=1, source_target_pairs={{0,1},{1,0},{2,3},{3,2},{4,5},{5,4},{6,7},{7,6},{8,9},{9,8},{10,11... | collective-permute-start | bytes 786440 | tf_op jit(solution)/shard_map/ppermute | solution.py:281
  36.0 8.4 %copy-start.9 = (bf16[128,768]{1,0:T(8,128)(2,1)}, bf16[128,768]{1,0:T(8,128)(2,1)S(1)}, u32[]{:S(2)}) copy-start(bf16[128,768]{1,0:T(8,128)(2,1)S(1)} %collective-permute-done.2.refs_1_) | copy-start | bytes 589828
  36.0 13.5 %collective-permute-start.4 = (bf16[128,768]{1,0:T(8,128)(2,1)S(1)}, bf16[128,768]{1,0:T(8,128)(2,1)S(1)}, u32[]{:S(2)}, u32[]{:S(2)}) collective-permute-start(bf16[128,768]{1,0:T(8,128)(2,1)S(1)} %collective-permute-done.2.refs_1_), channel_id=1, source_target_pairs={{0,2},{2,4},{4,6},{6,8},{8,10},{10,12},{12,14},{14,0},{1,3},{3,5},... | collective-permute-start | bytes 589832 | tf_op jit(solution)/shard_map/ppermute | solution.py:281
  40.6 3.8 %copy-start.10 = (bf16[128,768]{1,0:T(8,128)(2,1)}, bf16[128,768]{1,0:T(8,128)(2,1)S(1)}, u32[]{:S(2)}) copy-start(bf16[128,768]{1,0:T(8,128)(2,1)S(1)} %collective-permute-done.3.refs_2_) | copy-start | bytes 589828
  40.6 14.6 %collective-permute-start.5 = (bf16[128,768]{1,0:T(8,128)(2,1)S(1)}, bf16[128,768]{1,0:T(8,128)(2,1)S(1)}, u32[]{:S(2)}, u32[]{:S(2)}) collective-permute-start(bf16[128,768]{1,0:T(8,128)(2,1)S(1)} %collective-permute-done.3.refs_2_), channel_id=1, source_target_pairs={{0,14},{2,0},{4,2},{6,4},{8,6},{10,8},{12,10},{14,12},{1,15},{3,1}... | collective-permute-start | bytes 589832 | tf_op jit(solution)/shard_map/ppermute | solution.py:281
  44.9 47.2 %copy-start.4 = (bf16[64,2048]{1,0:T(8,128)(2,1)}, bf16[64,2048]{1,0:T(8,128)(2,1)S(1)}, u32[]{:S(2)}) copy-start(bf16[64,2048]{1,0:T(8,128)(2,1)S(1)} %collective-permute-done.1) | copy-start | bytes 786436
  49.5 28.5 %copy-start.11 = (bf16[128,768]{1,0:T(8,128)(2,1)}, bf16[128,768]{1,0:T(8,128)(2,1)S(1)}, u32[]{:S(2)}) copy-start(bf16[128,768]{1,0:T(8,128)(2,1)S(1)} %collective-permute-done.4.refs_3_) | copy-start | bytes 589828
  49.5 14.4 %collective-permute-start.6 = (bf16[128,768]{1,0:T(8,128)(2,1)S(1)}, bf16[128,768]{1,0:T(8,128)(2,1)S(1)}, u32[]{:S(2)}, u32[]{:S(2)}) collective-permute-start(bf16[128,768]{1,0:T(8,128)(2,1)S(1)} %collective-permute-done.4.refs_3_), channel_id=1, source_target_pairs={{0,2},{2,4},{4,6},{6,8},{8,10},{10,12},{12,14},{14,0},{1,3},{3,5},... | collective-permute-start | bytes 589832 | tf_op jit(solution)/shard_map/ppermute | solution.py:281
  55.2 22.8 %copy-start.12 = (bf16[128,768]{1,0:T(8,128)(2,1)}, bf16[128,768]{1,0:T(8,128)(2,1)S(1)}, u32[]{:S(2)}) copy-start(bf16[128,768]{1,0:T(8,128)(2,1)S(1)} %collective-permute-done.5.refs_4_) | copy-start | bytes 589828
  55.2 14.3 %collective-permute-start.7 = (bf16[128,768]{1,0:T(8,128)(2,1)S(1)}, bf16[128,768]{1,0:T(8,128)(2,1)S(1)}, u32[]{:S(2)}, u32[]{:S(2)}) collective-permute-start(bf16[128,768]{1,0:T(8,128)(2,1)S(1)} %collective-permute-done.5.refs_4_), channel_id=1, source_target_pairs={{0,14},{2,0},{4,2},{6,4},{8,6},{10,8},{12,10},{14,12},{1,15},{3,1}... | collective-permute-start | bytes 589832 | tf_op jit(solution)/shard_map/ppermute | solution.py:281
  63.9 14.1 %copy-start.6 = (bf16[128,768]{1,0:T(8,128)(2,1)}, bf16[128,768]{1,0:T(8,128)(2,1)S(1)}, u32[]{:S(2)}) copy-start(bf16[128,768]{1,0:T(8,128)(2,1)S(1)} %collective-permute-done.6.refs_5_) | copy-start | bytes 589828
  63.9 8.4 %collective-permute-start.8 = (bf16[64,768]{1,0:T(8,128)(2,1)S(1)}, bf16[64,768]{1,0:T(8,128)(2,1)S(1)}, u32[]{:S(2)}, u32[]{:S(2)}) collective-permute-start(bf16[64,768]{1,0:T(8,128)(2,1)S(1)} %slice.65), channel_id=1, source_target_pairs={{0,2},{2,4},{4,6},{6,8},{8,10},{10,12},{12,14},{14,0},{1,3},{3,5},... | collective-permute-start | bytes 294920 | tf_op jit(solution)/shard_map/ppermute | solution.py:281
  69.5 8.5 %copy-start.7 = (bf16[128,768]{1,0:T(8,128)(2,1)}, bf16[128,768]{1,0:T(8,128)(2,1)S(1)}, u32[]{:S(2)}) copy-start(bf16[128,768]{1,0:T(8,128)(2,1)S(1)} %collective-permute-done.7.refs_6_) | copy-start | bytes 589828
  69.6 7.7 %collective-permute-start.9 = (bf16[64,768]{1,0:T(8,128)(2,1)S(1)}, bf16[64,768]{1,0:T(8,128)(2,1)S(1)}, u32[]{:S(2)}, u32[]{:S(2)}) collective-permute-start(bf16[64,768]{1,0:T(8,128)(2,1)S(1)} %slice.66), channel_id=1, source_target_pairs={{0,14},{2,0},{4,2},{6,4},{8,6},{10,8},{12,10},{14,12},{1,15},{3,1}... | collective-permute-start | bytes 294920 | tf_op jit(solution)/shard_map/ppermute | solution.py:281
  108.9 14.7 %collective-permute-start.10 = (bf16[32,48,128]{2,1,0:T(8,128)(2,1)}, bf16[32,48,128]{2,1,0:T(8,128)(2,1)S(1)}, u32[]{:S(2)}, u32[]{:S(2)}) collective-permute-start(bf16[32,48,128]{2,1,0:T(8,128)(2,1)} %get-tuple-element.18), channel_id=1, source_target_pairs={{0,1},{1,0},{2,3},{3,2},{4,5},{5,4},{6,7},{7,6},{8,9},{9,8},{10,11... | collective-permute-start | bytes 1179656 | tf_op jit(solution)/shard_map/ppermute | solution.py:281
  123.6 0.8 copy-start.1
Sparse Core Ops, SparseCore 0:
  9.4 56.9 all-gather.1

commit v4 on v3

v4 whole, which is shorter than its diff:
```python
import functools

import jax
import jax.numpy as jnp
from jax import lax
from jax.experimental import pallas as pl
from jax.experimental.pallas import tpu as pltpu
from jax.sharding import Mesh
from jax.sharding import PartitionSpec as P

F32 = jnp.float32
BF16 = jnp.bfloat16
LOG2E = 1.4426950408889634
LIMIT = 2.0**64
ROWS = 80
BLOCK = 1024
PAY = 48
PLAIN = (((1,), (0,)), ((), ()))


def split(value):
    high = value.astype(BF16)
    return high, (value - high.astype(F32)).astype(BF16)


def attend_kernel(first, *refs):
    if first:
        x_ref, rstd_ref, w_ref, b_ref, q_ref, *refs = refs
        acc_refs, m_refs, (qa_ref, k_ref, v_ref) = refs[:2], refs[2:4], refs[4:]
    else:
        at_ref, x_ref, rstd_ref, w_ref, b_ref, q_ref, *refs = refs
        acc_ins, m_ins, pay_refs, refs = refs[:2], refs[2:4], refs[4:6], refs[6:]
        acc_refs, m_refs, (qa_ref, k_ref, v_ref, x_buf, sems) = refs[:2], refs[2:4], refs[4:]
    tokens = k_ref.shape[1]
    heads, size, latents = q_ref.shape
    block = 128
    steps = tokens // block

    def project(x, start, count):
        kv = jnp.dot(x, w_ref[...], preferred_element_type=F32)
        kv = (kv + b_ref[...]) * rstd_ref[pl.ds(start, count), :]
        lane = lax.broadcasted_iota(jnp.int32, (count, 2 * size), 1)
        for h in range(heads):
            mine = kv[:, 2 * size * h : 2 * size * (h + 1)].astype(BF16)
            k_ref[h, pl.ds(start, count), :] = jnp.where(lane < size, mine, jnp.ones_like(mine))
            v_ref[h, :size, pl.ds(start, count)] = mine.T[size:, :]

    for h in range(heads):
        v_ref[h, size:, :] = jnp.ones((ROWS - size, tokens), BF16)
        qa_ref[h, :size, :] = q_ref[h]
        qa_ref[h, size:, :] = jnp.zeros((size, latents), BF16)

    if first:
        project(x_ref[...], 0, tokens)
    else:
        pieces, count = x_buf.shape[:2]
        copies = []
        for t in range(pieces):
            place = lax.rem(at_ref[0] + t + 1, pieces + 1)
            rows = pl.ds(pl.multiple_of(place * count, count), count)
            copies.append(pltpu.make_async_copy(x_ref.at[rows], x_buf.at[t], sems.at[t]))
            copies[t].start()
        for t in range(pieces):
            copies[t].wait()
            project(x_buf[t], t * count, count)

    def scores(h, keys):
        return lax.dot_general(k_ref[h, keys, :], qa_ref[h], PLAIN, preferred_element_type=F32)

    def set_max(h, value):
        high, low = split(value)
        m_refs[h][...] = high.astype(F32) + low.astype(F32)
        qa_ref[h, size : size + 16, :] = jnp.concatenate(
            [-high, -low, jnp.zeros((14, latents), BF16)], axis=0
        )

    for h in range(heads):
        if first:
            set_max(h, jnp.max(scores(h, pl.ds(0, 128)), axis=0, keepdims=True))
        else:
            set_max(h, m_ins[h][...])

    def add(h, keys):
        probs = jnp.exp2(scores(h, keys)).astype(BF16)
        return lax.dot_general(v_ref[h, :, keys], probs, PLAIN, preferred_element_type=F32)

    for h in range(heads):
        acc_ref, m_ref = acc_refs[h], m_refs[h]
        for t in range(0, tokens, BLOCK):
            more = add(h, pl.ds(t, min(BLOCK, tokens - t)))
            if t > 0:
                acc_ref[...] += more
            else:
                acc_ref[...] = more if first else acc_ins[h][...] + more

        @pl.when(jnp.logical_not(jnp.max(acc_ref[size : size + 8, :]) < LIMIT))
        def _(h=h, acc_ref=acc_ref, m_ref=m_ref):
            before = m_ref[...]
            qa_ref[h, size:, :] = jnp.zeros((size, latents), BF16)

            def at(t):
                return pl.ds(pl.multiple_of(t * block, block), block)

            def widen(t, best):
                return jnp.maximum(best, jnp.max(scores(h, at(t)), axis=0, keepdims=True))

            set_max(h, lax.fori_loop(0, steps, widen, before))
            if first:
                acc_ref[...] = jnp.zeros((ROWS, latents), F32)
            else:
                acc_ref[...] = acc_ins[h][...] * jnp.exp2(before - m_ref[...])

            def redo(t, carry):
                acc_ref[...] += add(h, at(t))
                return carry

            lax.fori_loop(0, steps, redo, 0)

        if not first:
            for i in range(latents // 128):
                lanes = pl.ds(128 * i, 128)
                acc, total, m = acc_ref[:size, lanes], acc_ref[size : size + 1, lanes], m_ref[:, lanes]
                for side in range(2):
                    pay_refs[h][2 * i + side] = pack(fold_half(acc, side), both(total, side), both(m, side))


def both(row, side):
    lane = lax.broadcasted_iota(jnp.int32, row.shape, 1)
    keep = lane < 64 if side == 0 else lane >= 64
    return jnp.where(keep, row, pltpu.roll(row, 64, 1))


def fold_half(acc, side):
    half = acc.shape[0] // 2
    low, high = acc[:half], acc[half:]
    if side == 0:
        high = pltpu.roll(high, 64, 1)
    else:
        low = pltpu.roll(low, 64, 1)
    lane = lax.broadcasted_iota(jnp.int32, low.shape, 1)
    return jnp.where(lane < 64, low, high)


def pack(acc, total, m):
    t_high, m_high = total.astype(BF16).astype(F32), m.astype(BF16).astype(F32)
    fill = jnp.zeros((PAY - acc.shape[0] - 4, acc.shape[1]), F32)
    rows = [acc, t_high, total - t_high, m_high, m - m_high, fill]
    return jnp.concatenate(rows, axis=0).astype(BF16)


def attend(x, rstd, w, b, q, at=None, state=()):
    heads, size, latents = q.shape
    first = at is None
    vmem = pl.BlockSpec(memory_space=pltpu.VMEM)
    tokens = rstd.shape[0]
    accs = [jax.ShapeDtypeStruct((ROWS, latents), F32)] * heads
    ms = [jax.ShapeDtypeStruct((1, latents), F32)] * heads
    scratch = [
        pltpu.VMEM((heads, 2 * size, latents), BF16),
        pltpu.VMEM((heads, tokens, 2 * size), BF16),
        pltpu.VMEM((heads, ROWS, tokens), BF16),
    ]
    if first:
        ins, in_specs, out = (x, rstd, w, b, q), [vmem] * 5, accs + ms
    else:
        count = x.shape[0] - tokens
        ins = (at, x, rstd, w, b, q, *state)
        in_specs = [pl.BlockSpec(memory_space=pltpu.SMEM), pl.BlockSpec(memory_space=pl.ANY)]
        in_specs += [vmem] * (len(ins) - 2)
        out = [jax.ShapeDtypeStruct((latents // 64, PAY, 128), BF16)] * heads
        scratch = [pltpu.VMEM(i.shape, F32) for i in accs + ms] + scratch
        scratch += [
            pltpu.VMEM((tokens // count, count, x.shape[1]), BF16),
            pltpu.SemaphoreType.DMA((tokens // count,)),
        ]
    work = tokens * latents * heads
    return pl.pallas_call(
        functools.partial(attend_kernel, first),
        out_shape=out,
        in_specs=in_specs,
        out_specs=[vmem] * len(out),
        scratch_shapes=scratch,
        compiler_params=pltpu.CompilerParams(vmem_limit_bytes=56 << 20),
        cost_estimate=pl.CostEstimate(
            flops=16 * work * size, bytes_accessed=tokens * 1536, transcendentals=work
        ),
        name="attend",
    )(*ins)


def merge(parts):
    half = 32
    ms = [p[half + 2 : half + 3] + p[half + 3 : half + 4] for p in parts]
    top = functools.reduce(jnp.maximum, ms)
    acc, total = 0.0, 0.0
    for p, m in zip(parts, ms):
        factor = jnp.exp2(m - top)
        acc = acc + p[:half] * factor
        total = total + (p[half : half + 1] + p[half + 1 : half + 2]) * factor
    return acc, total, top


def combine_kernel(one_ref, two_ref, out_ref):
    for j in range(one_ref.shape[0]):
        out_ref[j] = pack(*merge([one_ref[j].astype(F32), two_ref[j].astype(F32)]))


def finish_kernel(last, parts_ref, out_ref):
    for j in range(parts_ref.shape[1]):
        merged = merge([parts_ref[i, j].astype(F32) for i in range(parts_ref.shape[0])])
        result = (merged[0] / merged[1]).astype(BF16) if last else pack(*merged)
        for i in range(out_ref.shape[0]):
            out_ref[i, j] = result


def combine(one, two):
    vmem = pl.BlockSpec(memory_space=pltpu.VMEM)
    return pl.pallas_call(
        combine_kernel,
        out_shape=jax.ShapeDtypeStruct(one.shape, BF16),
        in_specs=[vmem] * 2,
        out_specs=vmem,
        name="combine",
    )(one, two)


def finish(parts, copies, last):
    vmem = pl.BlockSpec(memory_space=pltpu.VMEM)
    return pl.pallas_call(
        functools.partial(finish_kernel, last),
        out_shape=jax.ShapeDtypeStruct((copies, parts.shape[1], 32 if last else PAY, 128), BF16),
        in_specs=[vmem],
        out_specs=vmem,
        name="finish",
    )(parts)


def place_kernel(parts_ref, out_ref):
    half = parts_ref.shape[1]
    for i in range(parts_ref.shape[0] // 2):
        one, two = parts_ref[2 * i].astype(F32), parts_ref[2 * i + 1].astype(F32)
        lane = lax.broadcasted_iota(jnp.int32, one.shape, 1)
        low = jnp.where(lane < 64, one, pltpu.roll(two, 64, 1))
        high = jnp.where(lane < 64, pltpu.roll(one, 64, 1), two)
        out_ref[:half, pl.ds(128 * i, 128)] = low.astype(BF16)
        out_ref[half:, pl.ds(128 * i, 128)] = high.astype(BF16)


def place(parts):
    vmem = pl.BlockSpec(memory_space=pltpu.VMEM)
    return pl.pallas_call(
        place_kernel,
        out_shape=jax.ShapeDtypeStruct((64, 64 * parts.shape[0]), BF16),
        in_specs=[vmem],
        out_specs=vmem,
        name="place",
    )(parts)


def exchange(parts, axis):
    return lax.all_to_all(parts, axis, split_axis=0, concat_axis=0, tiled=True)


def shift(block, axis, by):
    size = lax.axis_size(axis)
    return lax.ppermute(block, axis, [(i, (i + by) % size) for i in range(size)])


def body(patches, w_patch, patch_bias, w_kv, queries):
    size = queries.shape[1]
    tokens = patches.shape[0]
    gathered = lax.all_gather(patches, "z", axis=0, tiled=True)

    weight = w_patch.astype(F32)
    weight = weight - jnp.mean(weight, axis=1, keepdims=True)
    bias = patch_bias - jnp.mean(patch_bias)
    embed = jnp.dot(patches, w_patch, preferred_element_type=F32) + patch_bias
    mean = jnp.mean(embed, axis=-1, keepdims=True)
    var = jnp.mean((embed - mean) * (embed - mean), axis=-1)
    rstd = lax.rsqrt(var + 1e-05)
    mine = rstd.reshape(-1, 1)
    rstd = exchange(jnp.broadcast_to(rstd[None], (lax.axis_size("z"), tokens)), "z")
    at = lax.axis_index("z")
    turned = lax.dynamic_slice_in_dim(jnp.concatenate([rstd, rstd]), at + 1, rstd.shape[0] - 1, axis=0)

    w_pair = jnp.stack([shift(w_kv, "c", 1), w_kv])
    q_pair = jnp.stack([shift(queries.T, "c", 1), queries.T])
    scale = jnp.where(jnp.arange(2 * size) < size, LOG2E * float(size) ** (-0.5), 1.0)
    fold = jnp.einsum("pd,hdn->hpn", weight, w_pair.astype(F32), precision=lax.Precision.HIGHEST)
    fold = (fold * scale).astype(BF16)
    fold_bias = jnp.einsum("d,hdn->hn", bias, w_pair.astype(F32), precision=lax.Precision.HIGHEST)
    fold_bias = fold_bias * scale

    weights = (jnp.concatenate([fold[0], fold[1]], axis=1), fold_bias.reshape(1, -1), q_pair)
    state = attend(patches, mine, *weights)
    other, own = attend(gathered, turned.reshape(-1, 1), *weights, at.reshape(1), state)

    with jax.named_scope("totals"):
        part = combine(own, shift(other, "c", 1))
        part = exchange(part.reshape(lax.axis_size("y"), -1, PAY, 128), "y")
        part = exchange(finish(part, lax.axis_size("x"), False), "x")
    with jax.named_scope("readout"):
        part = exchange(finish(part, lax.axis_size("y"), True), "y")
        return place(part.reshape(-1, 32, 128)).T


def solution(mesh):
    grid = Mesh(mesh.devices.reshape(8, 4, 8, 2), ("y", "x", "z", "c"))
    head = P(None, ("z", "c"))
    placed = (P(("y", "x", "z", "c"), None), P(), P(), head, head)
    return jax.shard_map(body, mesh=grid, in_specs=placed, out_specs=head, check_vma=False)
```

time: 180 us -> 193 us (1.072)
  the two profiles are of different devices: /device:TPU:192 before, /device:TPU:2 now
where the time goes in v4:
time: 193 us; the launch traced here: 192 us
  Pallas kernels  65.3 us (34%)
  blocking collectives  46.1 us (24%)
  waiting for transfers between devices  37.2 us (19%)
  starting transfers between devices  16.6 us (9%)
  between operations  14.2 us (7%)
  local copies, waits for them, and re-layouts  4.9 us (3%)
  matrix products  4.68 us (2%)
  other arithmetic  3.44 us (2%)
    pallas_call x2, Pallas kernels, attend(): pl.pallas_call(functools.partial(attend_kernel, first), out_shape=out, in...  57.9 us
    all_to_all x3, blocking collectives, exchange(): return lax.all_to_all(parts, axis, split_axis=0, concat_axis=0, tiled=True)  46.1 us
    all_gather x1, waiting for transfers between devices, body(): gathered = lax.all_gather(patches, 'z', axis=0, tiled=True)  29.1 us
    all_to_all x1, starting transfers between devices, exchange(): return lax.all_to_all(parts, axis, split_axis=0, concat_axis=0, tiled=True)  10.3 us
    ppermute x3, starting transfers between devices, shift(): lax.ppermute(block, axis, [(i, (i + by) % size) for i in range(size)])  6.25 us
    all_to_all x1, waiting for transfers between devices, exchange(): return lax.all_to_all(parts, axis, split_axis=0, concat_axis=0, tiled=True)  5.48 us
  transfers between devices with their start and end apart: 5, of which 3 were waited for; matrix products, arithmetic and copies ran while one was open for 6% of the time, Pallas kernels for 4%

profile of v4, /device:TPU:2, one launch (start us, length us, event | category | flops | bytes accessed | tf_op | source)
XLA Modules:
  0.0 192.5 jit_solution(16048471588709089801)
XLA Ops:
  6.5 0.0 all-gather.2.cloned.1.call-start
  6.5 0.7 all-gather.2.cloned.1.call-update
  7.3 1.1 copy.14
  8.3 1.9 collective-permute-start
  10.3 2.4 %collective-permute-start.1 = (bf16[64,2048]{1,0:T(8,128)(2,1)}, bf16[64,2048]{1,0:T(8,128)(2,1)S(1)}, u32[]{:S(2)}, u32[]{:S(2)}) collective-permute-start(bf16[64,2048]{1,0:T(8,128)(2,1)} %bitcast.49), channel_id=1, source_target_pairs={{0,1},{1,0},{2,3},{3,2},{4,5},{5,4},{6,7},{7,6},{8,9},{9,8},{10,11... | collective-permute-start | bytes 786440 | tf_op jit(solution)/shard_map/ppermute | solution.py:266
  12.7 2.4 %fusion.15 = (f32[384]{0:T(512)S(1)}, f32[384,1024]{1,0:T(8,128)S(1)}) fusion(f32[1024]{0:T(1024)} %param.7, bf16[384,768]{1,0:T(8,128)(2,1)} %refs_0_.1, bf16[768,1024]{1,0:T(8,128)(2,1)} %param.6), kind=kOutput, calls=%fused_computation.26 | convolution fusion | flops 604765824 | bytes 3741184 | tf_op jit(solution)/shard_map/dot_general | solution.py:277
  15.1 0.0 copy-start.3
  15.1 0.0 copy-start
  15.1 0.3 multiply_reduce_fusion
  15.4 0.6 broadcast_in_dim.8
  16.1 10.3 %all-to-all-start = ((f32[8,1,384]{2,1,0:T(1,128)}), f32[8,1,384]{2,1,0:T(1,128)S(1)}, u32[]{:S(2)}, u32[]{:S(2)}) async-start(f32[8,1,384]{2,1,0:T(1,128)} %broadcast_in_dim.8), calls=%async_computation | async-start | bytes 24576 | tf_op jit(solution)/shard_map/all_to_all | solution.py:261
  26.4 0.0 copy-done.3
  26.4 0.6 reduce_sum.39
  27.6 0.0 copy-done
  27.6 0.3 convert_reduce_fusion
  27.9 0.8 rsqrt.19.refs_1_
  28.7 5.5 %all-to-all-done = f32[8,1,384]{2,1,0:T(1,128)S(1)} async-done(((f32[8,1,384]{2,1,0:T(1,128)}), f32[8,1,384]{2,1,0:T(1,128)S(1)}, u32[]{:S(2)}, u32[]{:S(2)}) %all-to-all-start) | async-done | bytes 12320 | tf_op jit(solution)/shard_map/all_to_all | solution.py:261
  34.3 1.6 copy.22
  35.8 0.0 collective-permute-done
  35.9 0.1 pad_maximum_fusion
  35.9 0.5 fusion.16
  36.4 1.8 fusion.10
  38.2 0.0 copy-start.2
  38.2 0.8 pad_maximum_fusion.2.refs_2_.refs_3_
  39.1 0.5 broadcast_multiply_fusion.2
  39.6 0.0 collective-permute-done.1
  39.6 0.0 copy-done.2
  39.6 0.8 pad_maximum_fusion.1.refs_4_.refs_5_
  40.4 7.7 %attend.2 = (f32[80,2048]{1,0:T(8,128)}, f32[80,2048]{1,0:T(8,128)}, f32[1,2048]{1,0:T(1,128)}, f32[1,2048]{1,0:T(1,128)}) custom-call(bf16[384,768]{1,0:T(8,128)(2,1)} %refs_0_.1, f32[384,1]{1,0:T(8,128)} %rsqrt.19.refs_1_, bf16[768,256]{1,0:T(8,128)(2,1)} %pad_maximum_fusion.2.refs_2_.refs_3_, f32[1,256]{1,0:T(1,128)} %bitcast.58, ...), custom_call_target="tpu_custom_call" | custom-call | flops 1610612736 | bytes 589824 | tf_op jit(solution)/shard_map/attend/pallas_call | solution.py:177
  48.2 29.1 %all-gather.2.cloned.1.call-done.refs_1_ = bf16[3072,768]{1,0:T(8,128)(2,1)} async-done(((bf16[384,768]{1,0:T(8,128)(2,1)}), bf16[3072,768]{1,0:T(8,128)(2,1)}) %all-gather.2.cloned.1.call-update) | async-done | bytes 4718608 | tf_op jit(solution)/shard_map/all_gather | solution.py:272
  77.3 50.2 %attend.3 = (bf16[32,48,128]{2,1,0:T(8,128)(2,1)}, bf16[32,48,128]{2,1,0:T(8,128)(2,1)}) custom-call(s32[1]{0:T(128)} %bitcast.refs_0_, bf16[3072,768]{1,0:T(8,128)(2,1)} %all-gather.2.cloned.1.call-done.refs_1_, f32[2688,1]{1,0:T(8,128)} %bitcast.45, bf16[768,256]{1,0:T(8,128)(2,1)} %pad_maximum_fusion.2.refs_2_.refs_3_, f32[1,256]{1,0:T(1,128)} %bitcast.59, ...), custom_call_target="tpu_custom_call" | custom-call | flops 11274289152 | bytes 4128768 | tf_op jit(solution)/shard_map/attend/pallas_call | solution.py:177
  127.5 1.9 collective-permute-start.2
  129.4 1.9 collective-permute-done.2.two_ref
  131.3 0.0 copy-start.1
  131.3 0.8 copy-done.1
  132.1 2.1 %combine.1 = bf16[32,48,128]{2,1,0:T(8,128)(2,1)} custom-call(bf16[32,48,128]{2,1,0:T(8,128)(2,1)} %get-tuple-element.15.one_ref, bf16[32,48,128]{2,1,0:T(8,128)(2,1)} %copy-done.1), custom_call_target="tpu_custom_call" | custom-call | tf_op jit(solution)/shard_map/totals/combine/pallas_call | solution.py:218
  134.2 21.9 %all_to_all.24.parts_ref = bf16[8,4,48,128]{3,2,1,0:T(8,128)(2,1)} all-to-all(bf16[8,4,48,128]{3,2,1,0:T(8,128)(2,1)} %bitcast.44), channel_id=1, replica_groups=mesh['y'=8,'x'=4,'z'=8,'c'=2] {'y'}, dimensions={0} | all-to-all | bytes 786432 | tf_op jit(solution)/shard_map/totals/all_to_all | solution.py:261
  156.1 1.8 finish.2
  157.9 9.8 %all_to_all.25.parts_ref = bf16[4,4,48,128]{3,2,1,0:T(8,128)(2,1)} all-to-all(bf16[4,4,48,128]{3,2,1,0:T(8,128)(2,1)} %finish.2), channel_id=1, replica_groups=mesh['y'=8,'x'=4,'z'=8,'c'=2] {'x'}, dimensions={0} | all-to-all | bytes 393216 | tf_op jit(solution)/shard_map/totals/all_to_all | solution.py:261
  167.6 1.7 finish.3
  169.3 14.5 %all_to_all.26 = bf16[8,4,32,128]{3,2,1,0:T(8,128)(2,1)} all-to-all(bf16[8,4,32,128]{3,2,1,0:T(8,128)(2,1)} %finish.3), channel_id=1, replica_groups=mesh['y'=8,'x'=4,'z'=8,'c'=2] {'y'}, dimensions={0} | all-to-all | bytes 524288 | tf_op jit(solution)/shard_map/readout/all_to_all | solution.py:261
  183.8 1.8 place.1
  (9 shorter events, 0.1 us)
Async XLA Ops:
  6.5 70.8 %all-gather.2.cloned.1.call-start = ((), (), s32[]{:S(2)}) async-start(), calls=%async_computation.4 | async-start | bytes 5308416 | tf_op jit(solution)/shard_map/all_gather | solution.py:272
  8.3 27.5 %collective-permute-start = (bf16[1024,128]{0,1:T(8,128)(2,1)S(1)}, bf16[1024,128]{0,1:T(8,128)(2,1)S(1)}, u32[]{:S(2)}, u32[]{:S(2)}) collective-permute-start(bf16[1024,128]{0,1:T(8,128)(2,1)S(1)} %copy.14), channel_id=1, source_target_pairs={{0,1},{1,0},{2,3},{3,2},{4,5},{5,4},{6,7},{7,6},{8,9},{9,8},{10,11... | collective-permute-start | bytes 786440 | tf_op jit(solution)/shard_map/ppermute | solution.py:266
  10.3 29.3 %collective-permute-start.1 = (bf16[64,2048]{1,0:T(8,128)(2,1)}, bf16[64,2048]{1,0:T(8,128)(2,1)S(1)}, u32[]{:S(2)}, u32[]{:S(2)}) collective-permute-start(bf16[64,2048]{1,0:T(8,128)(2,1)} %bitcast.49), channel_id=1, source_target_pairs={{0,1},{1,0},{2,3},{3,2},{4,5},{5,4},{6,7},{7,6},{8,9},{9,8},{10,11... | collective-permute-start | bytes 786440 | tf_op jit(solution)/shard_map/ppermute | solution.py:266
  15.1 11.3 %copy-start.3 = (f32[1024]{0:T(1024)S(1)}, f32[1024]{0:T(1024)}, u32[]{:S(2)}) copy-start(f32[1024]{0:T(1024)} %param.7) | copy-start | bytes 12292
  15.1 12.5 %copy-start = (bf16[768,1024]{1,0:T(8,128)(2,1)S(1)}, bf16[768,1024]{1,0:T(8,128)(2,1)}, u32[]{:S(2)}) copy-start(bf16[768,1024]{1,0:T(8,128)(2,1)} %param.6) | copy-start | bytes 4718596
  16.1 18.2 %all-to-all-start = ((f32[8,1,384]{2,1,0:T(1,128)}), f32[8,1,384]{2,1,0:T(1,128)S(1)}, u32[]{:S(2)}, u32[]{:S(2)}) async-start(f32[8,1,384]{2,1,0:T(1,128)} %broadcast_in_dim.8), calls=%async_computation | async-start | bytes 24576 | tf_op jit(solution)/shard_map/all_to_all | solution.py:261
  38.2 1.4 copy-start.2
  127.5 3.8 %collective-permute-start.2 = (bf16[32,48,128]{2,1,0:T(8,128)(2,1)}, bf16[32,48,128]{2,1,0:T(8,128)(2,1)S(1)}, u32[]{:S(2)}, u32[]{:S(2)}) collective-permute-start(bf16[32,48,128]{2,1,0:T(8,128)(2,1)} %get-tuple-element.16), channel_id=1, source_target_pairs={{0,1},{1,0},{2,3},{3,2},{4,5},{5,4},{6,7},{7,6},{8,9},{9,8},{10,11... | collective-permute-start | bytes 1179656 | tf_op jit(solution)/shard_map/totals/ppermute | solution.py:266
  131.3 0.8 copy-start.1
Sparse Core Ops, SparseCore 0:
  9.4 67.8 all-gather.1

commit v5 on v4

--- a/solution.py
+++ b/solution.py
@@ -14,7 +14,7 @@
 LIMIT = 2.0**64
 ROWS = 80
 BLOCK = 1024
-PAY = 48
+PAY = 40
 PLAIN = (((1,), (0,)), ((), ()))
 
 
@@ -36,6 +36,15 @@
     block = 128
     steps = tokens // block
 
+    if not first:
+        pieces, count = x_buf.shape[:2]
+        copies = []
+        for t in range(pieces):
+            place = lax.rem(at_ref[0] + t + 1, pieces + 1)
+            rows = pl.ds(pl.multiple_of(place * count, count), count)
+            copies.append(pltpu.make_async_copy(x_ref.at[rows], x_buf.at[t], sems.at[t]))
+            copies[t].start()
+
     def project(x, start, count):
         kv = jnp.dot(x, w_ref[...], preferred_element_type=F32)
         kv = (kv + b_ref[...]) * rstd_ref[pl.ds(start, count), :]
@@ -53,13 +62,6 @@
     if first:
         project(x_ref[...], 0, tokens)
     else:
-        pieces, count = x_buf.shape[:2]
-        copies = []
-        for t in range(pieces):
-            place = lax.rem(at_ref[0] + t + 1, pieces + 1)
-            rows = pl.ds(pl.multiple_of(place * count, count), count)
-            copies.append(pltpu.make_async_copy(x_ref.at[rows], x_buf.at[t], sems.at[t]))
-            copies[t].start()
         for t in range(pieces):
             copies[t].wait()
             project(x_buf[t], t * count, count)
@@ -205,12 +207,11 @@
         out_ref[j] = pack(*merge([one_ref[j].astype(F32), two_ref[j].astype(F32)]))
 
 
-def finish_kernel(last, parts_ref, out_ref):
-    for j in range(parts_ref.shape[1]):
-        merged = merge([parts_ref[i, j].astype(F32) for i in range(parts_ref.shape[0])])
-        result = (merged[0] / merged[1]).astype(BF16) if last else pack(*merged)
-        for i in range(out_ref.shape[0]):
-            out_ref[i, j] = result
+def finish_kernel(parts_ref, out_ref):
+    acc, total, _ = merge([parts_ref[i].astype(F32) for i in range(parts_ref.shape[0])])
+    result = (acc / total).astype(BF16)
+    for i in range(out_ref.shape[0]):
+        out_ref[i] = result
 
 
 def combine(one, two):
@@ -224,11 +225,11 @@
     )(one, two)
 
 
-def finish(parts, copies, last):
+def finish(parts, copies):
     vmem = pl.BlockSpec(memory_space=pltpu.VMEM)
     return pl.pallas_call(
-        functools.partial(finish_kernel, last),
-        out_shape=jax.ShapeDtypeStruct((copies, parts.shape[1], 32 if last else PAY, 128), BF16),
+        finish_kernel,
+        out_shape=jax.ShapeDtypeStruct((copies, 32, 128), BF16),
         in_specs=[vmem],
         out_specs=vmem,
         name="finish",
@@ -296,12 +297,10 @@
     other, own = attend(gathered, turned.reshape(-1, 1), *weights, at.reshape(1), state)
 
     with jax.named_scope("totals"):
-        part = combine(own, shift(other, "c", 1))
-        part = exchange(part.reshape(lax.axis_size("y"), -1, PAY, 128), "y")
-        part = exchange(finish(part, lax.axis_size("x"), False), "x")
+        part = exchange(combine(own, shift(other, "c", 1)), ("y", "x"))
+        part = finish(part, part.shape[0])
     with jax.named_scope("readout"):
-        part = exchange(finish(part, lax.axis_size("y"), True), "y")
-        return place(part.reshape(-1, 32, 128)).T
+        return place(exchange(part, ("y", "x"))).T
 
 
 def solution(mesh):

time: 193 us -> 185 us (0.959)
  the two profiles are of different devices: /device:TPU:2 before, /device:TPU:8 now
where the time goes in v5:
time: 185 us; the launch traced here: 184 us
  Pallas kernels  63.5 us (34%)
  blocking collectives  40 us (22%)
  waiting for transfers between devices  37 us (20%)
  starting transfers between devices  16.6 us (9%)
  between operations  14.2 us (8%)
  local copies, waits for them, and re-layouts  4.88 us (3%)
  matrix products  4.68 us (3%)
  other arithmetic  3.49 us (2%)
    pallas_call x2, Pallas kernels, attend(): pl.pallas_call(functools.partial(attend_kernel, first), out_shape=out, in...  57.9 us
    all_to_all x2, blocking collectives, exchange(): return lax.all_to_all(parts, axis, split_axis=0, concat_axis=0, tiled=True)  40 us
    all_gather x1, waiting for transfers between devices, body(): gathered = lax.all_gather(patches, 'z', axis=0, tiled=True)  29 us
    all_to_all x1, starting transfers between devices, exchange(): return lax.all_to_all(parts, axis, split_axis=0, concat_axis=0, tiled=True)  10.3 us
    ppermute x3, starting transfers between devices, shift(): lax.ppermute(block, axis, [(i, (i + by) % size) for i in range(size)])  6.28 us
    all_to_all x1, waiting for transfers between devices, exchange(): return lax.all_to_all(parts, axis, split_axis=0, concat_axis=0, tiled=True)  5.48 us
  transfers between devices with their start and end apart: 5, of which 3 were waited for; matrix products, arithmetic and copies ran while one was open for 7% of the time, Pallas kernels for 4%

profile of v5, /device:TPU:8, one launch (start us, length us, event | category | flops | bytes accessed | tf_op | source)
XLA Modules:
  0.0 184.3 jit_solution(14832805494009431850)
XLA Ops:
  6.5 0.0 all-gather.2.cloned.1.call-start
  6.5 0.7 all-gather.2.cloned.1.call-update
  7.3 1.1 copy.14
  8.3 1.9 %collective-permute-start = (bf16[1024,128]{0,1:T(8,128)(2,1)S(1)}, bf16[1024,128]{0,1:T(8,128)(2,1)S(1)}, u32[]{:S(2)}, u32[]{:S(2)}) collective-permute-start(bf16[1024,128]{0,1:T(8,128)(2,1)S(1)} %copy.14), channel_id=1, source_target_pairs={{0,1},{1,0},{2,3},{3,2},{4,5},{5,4},{6,7},{7,6},{8,9},{9,8},{10,11... | collective-permute-start | bytes 786440 | tf_op jit(solution)/shard_map/ppermute | solution.py:267
  10.3 2.4 %collective-permute-start.1 = (bf16[64,2048]{1,0:T(8,128)(2,1)}, bf16[64,2048]{1,0:T(8,128)(2,1)S(1)}, u32[]{:S(2)}, u32[]{:S(2)}) collective-permute-start(bf16[64,2048]{1,0:T(8,128)(2,1)} %bitcast.45), channel_id=1, source_target_pairs={{0,1},{1,0},{2,3},{3,2},{4,5},{5,4},{6,7},{7,6},{8,9},{9,8},{10,11... | collective-permute-start | bytes 786440 | tf_op jit(solution)/shard_map/ppermute | solution.py:267
  12.7 2.4 %fusion.15 = (f32[384]{0:T(512)S(1)}, f32[384,1024]{1,0:T(8,128)S(1)}) fusion(f32[1024]{0:T(1024)} %param.7, bf16[384,768]{1,0:T(8,128)(2,1)} %refs_0_.1, bf16[768,1024]{1,0:T(8,128)(2,1)} %param.6), kind=kOutput, calls=%fused_computation.26 | convolution fusion | flops 604765824 | bytes 3741184 | tf_op jit(solution)/shard_map/dot_general | solution.py:278
  15.1 0.0 copy-start.3
  15.1 0.0 copy-start
  15.1 0.3 multiply_reduce_fusion
  15.4 0.6 broadcast_in_dim.8
  16.1 10.3 %all-to-all-start = ((f32[8,1,384]{2,1,0:T(1,128)}), f32[8,1,384]{2,1,0:T(1,128)S(1)}, u32[]{:S(2)}, u32[]{:S(2)}) async-start(f32[8,1,384]{2,1,0:T(1,128)} %broadcast_in_dim.8), calls=%async_computation | async-start | bytes 24576 | tf_op jit(solution)/shard_map/all_to_all | solution.py:262
  26.4 0.0 copy-done.3
  26.4 0.6 reduce_sum.39
  27.6 0.0 copy-done
  27.6 0.3 convert_reduce_fusion
  27.9 0.8 rsqrt.19.refs_1_
  28.7 5.5 %all-to-all-done = f32[8,1,384]{2,1,0:T(1,128)S(1)} async-done(((f32[8,1,384]{2,1,0:T(1,128)}), f32[8,1,384]{2,1,0:T(1,128)S(1)}, u32[]{:S(2)}, u32[]{:S(2)}) %all-to-all-start) | async-done | bytes 12320 | tf_op jit(solution)/shard_map/all_to_all | solution.py:262
  34.3 1.6 copy.22
  35.8 0.0 collective-permute-done
  35.9 0.1 pad_maximum_fusion
  35.9 0.5 fusion.16
  36.4 1.8 fusion.10
  38.2 0.0 copy-start.2
  38.2 0.8 pad_maximum_fusion.2.refs_2_.refs_3_
  39.1 0.6 broadcast_multiply_fusion.2
  39.6 0.0 collective-permute-done.1
  39.6 0.0 copy-done.2
  39.6 0.8 pad_maximum_fusion.1.refs_4_.refs_5_
  40.5 7.8 %attend.2 = (f32[80,2048]{1,0:T(8,128)}, f32[80,2048]{1,0:T(8,128)}, f32[1,2048]{1,0:T(1,128)}, f32[1,2048]{1,0:T(1,128)}) custom-call(bf16[384,768]{1,0:T(8,128)(2,1)} %refs_0_.1, f32[384,1]{1,0:T(8,128)} %rsqrt.19.refs_1_, bf16[768,256]{1,0:T(8,128)(2,1)} %pad_maximum_fusion.2.refs_2_.refs_3_, f32[1,256]{1,0:T(1,128)} %bitcast.54, ...), custom_call_target="tpu_custom_call" | custom-call | flops 1610612736 | bytes 589824 | tf_op jit(solution)/shard_map/attend/pallas_call | solution.py:179
  48.2 29.0 %all-gather.2.cloned.1.call-done.refs_1_ = bf16[3072,768]{1,0:T(8,128)(2,1)} async-done(((bf16[384,768]{1,0:T(8,128)(2,1)}), bf16[3072,768]{1,0:T(8,128)(2,1)}) %all-gather.2.cloned.1.call-update) | async-done | bytes 4718608 | tf_op jit(solution)/shard_map/all_gather | solution.py:273
  77.3 50.1 %attend.3 = (bf16[32,40,128]{2,1,0:T(8,128)(2,1)}, bf16[32,40,128]{2,1,0:T(8,128)(2,1)}) custom-call(s32[1]{0:T(128)} %bitcast.refs_0_, bf16[3072,768]{1,0:T(8,128)(2,1)} %all-gather.2.cloned.1.call-done.refs_1_, f32[2688,1]{1,0:T(8,128)} %bitcast.42, bf16[768,256]{1,0:T(8,128)(2,1)} %pad_maximum_fusion.2.refs_2_.refs_3_, f32[1,256]{1,0:T(1,128)} %bitcast.55, ...), custom_call_target="tpu_custom_call" | custom-call | flops 11274289152 | bytes 4128768 | tf_op jit(solution)/shard_map/attend/pallas_call | solution.py:179
  127.4 2.0 %collective-permute-start.2 = (bf16[32,40,128]{2,1,0:T(8,128)(2,1)}, bf16[32,40,128]{2,1,0:T(8,128)(2,1)S(1)}, u32[]{:S(2)}, u32[]{:S(2)}) collective-permute-start(bf16[32,40,128]{2,1,0:T(8,128)(2,1)} %get-tuple-element.16), channel_id=1, source_target_pairs={{0,1},{1,0},{2,3},{3,2},{4,5},{5,4},{6,7},{7,6},{8,9},{9,8},{10,11... | collective-permute-start | bytes 983048 | tf_op jit(solution)/shard_map/totals/ppermute | solution.py:267
  129.3 1.8 collective-permute-done.2.two_ref
  131.1 0.0 copy-start.1
  131.1 0.7 copy-done.1
  131.8 2.0 %combine.1 = bf16[32,40,128]{2,1,0:T(8,128)(2,1)} custom-call(bf16[32,40,128]{2,1,0:T(8,128)(2,1)} %get-tuple-element.15.one_ref, bf16[32,40,128]{2,1,0:T(8,128)(2,1)} %copy-done.1), custom_call_target="tpu_custom_call" | custom-call | tf_op jit(solution)/shard_map/totals/combine/pallas_call | solution.py:219
  133.9 23.7 %all_to_all.19.parts_ref = bf16[32,40,128]{2,1,0:T(8,128)(2,1)} all-to-all(bf16[32,40,128]{2,1,0:T(8,128)(2,1)} %combine.1), channel_id=1, replica_groups=mesh['y'=8,'x'=4,'z'=8,'c'=2] {'y','x'}, dimensions={0} | all-to-all | bytes 655360 | tf_op jit(solution)/shard_map/totals/all_to_all | solution.py:262
  157.6 1.8 finish.1
  159.4 16.3 %all_to_all.20.parts_ref = bf16[32,32,128]{2,1,0:T(8,128)(2,1)} all-to-all(bf16[32,32,128]{2,1,0:T(8,128)(2,1)} %finish.1), channel_id=1, replica_groups=mesh['y'=8,'x'=4,'z'=8,'c'=2] {'y','x'}, dimensions={0} | all-to-all | bytes 524288 | tf_op jit(solution)/shard_map/readout/all_to_all | solution.py:262
  175.7 1.8 place.1
  (9 shorter events, 0.1 us)
Async XLA Ops:
  6.5 70.7 %all-gather.2.cloned.1.call-start = ((), (), s32[]{:S(2)}) async-start(), calls=%async_computation.3 | async-start | bytes 5308416 | tf_op jit(solution)/shard_map/all_gather | solution.py:273
  8.3 27.5 %collective-permute-start = (bf16[1024,128]{0,1:T(8,128)(2,1)S(1)}, bf16[1024,128]{0,1:T(8,128)(2,1)S(1)}, u32[]{:S(2)}, u32[]{:S(2)}) collective-permute-start(bf16[1024,128]{0,1:T(8,128)(2,1)S(1)} %copy.14), channel_id=1, source_target_pairs={{0,1},{1,0},{2,3},{3,2},{4,5},{5,4},{6,7},{7,6},{8,9},{9,8},{10,11... | collective-permute-start | bytes 786440 | tf_op jit(solution)/shard_map/ppermute | solution.py:267
  10.3 29.4 %collective-permute-start.1 = (bf16[64,2048]{1,0:T(8,128)(2,1)}, bf16[64,2048]{1,0:T(8,128)(2,1)S(1)}, u32[]{:S(2)}, u32[]{:S(2)}) collective-permute-start(bf16[64,2048]{1,0:T(8,128)(2,1)} %bitcast.45), channel_id=1, source_target_pairs={{0,1},{1,0},{2,3},{3,2},{4,5},{5,4},{6,7},{7,6},{8,9},{9,8},{10,11... | collective-permute-start | bytes 786440 | tf_op jit(solution)/shard_map/ppermute | solution.py:267
  15.1 11.3 %copy-start.3 = (f32[1024]{0:T(1024)S(1)}, f32[1024]{0:T(1024)}, u32[]{:S(2)}) copy-start(f32[1024]{0:T(1024)} %param.7) | copy-start | bytes 12292
  15.1 12.5 %copy-start = (bf16[768,1024]{1,0:T(8,128)(2,1)S(1)}, bf16[768,1024]{1,0:T(8,128)(2,1)}, u32[]{:S(2)}) copy-start(bf16[768,1024]{1,0:T(8,128)(2,1)} %param.6) | copy-start | bytes 4718596
  16.1 18.2 %all-to-all-start = ((f32[8,1,384]{2,1,0:T(1,128)}), f32[8,1,384]{2,1,0:T(1,128)S(1)}, u32[]{:S(2)}, u32[]{:S(2)}) async-start(f32[8,1,384]{2,1,0:T(1,128)} %broadcast_in_dim.8), calls=%async_computation | async-start | bytes 24576 | tf_op jit(solution)/shard_map/all_to_all | solution.py:262
  38.2 1.5 copy-start.2
  127.4 3.7 %collective-permute-start.2 = (bf16[32,40,128]{2,1,0:T(8,128)(2,1)}, bf16[32,40,128]{2,1,0:T(8,128)(2,1)S(1)}, u32[]{:S(2)}, u32[]{:S(2)}) collective-permute-start(bf16[32,40,128]{2,1,0:T(8,128)(2,1)} %get-tuple-element.16), channel_id=1, source_target_pairs={{0,1},{1,0},{2,3},{3,2},{4,5},{5,4},{6,7},{7,6},{8,9},{9,8},{10,11... | collective-permute-start | bytes 983048 | tf_op jit(solution)/shard_map/totals/ppermute | solution.py:267
  131.1 0.7 copy-start.1
Sparse Core Ops, SparseCore 0:
  9.4 67.7 all-gather.1

commit v6 on v5

--- a/solution.py
+++ b/solution.py
@@ -30,7 +30,7 @@
     else:
         at_ref, x_ref, rstd_ref, w_ref, b_ref, q_ref, *refs = refs
         acc_ins, m_ins, pay_refs, refs = refs[:2], refs[2:4], refs[4:6], refs[6:]
-        acc_refs, m_refs, (qa_ref, k_ref, v_ref, x_buf, sems) = refs[:2], refs[2:4], refs[4:]
+        acc_refs, m_refs, (qa_ref, k_ref, v_ref, x_buf, sems, acc_bufs, acc_sems) = refs[:2], refs[2:4], refs[4:]
     tokens = k_ref.shape[1]
     heads, size, latents = q_ref.shape
     block = 128
@@ -44,13 +44,18 @@
             rows = pl.ds(pl.multiple_of(place * count, count), count)
             copies.append(pltpu.make_async_copy(x_ref.at[rows], x_buf.at[t], sems.at[t]))
             copies[t].start()
+        sums = [pltpu.make_async_copy(acc_ins[h], acc_bufs.at[h], acc_sems.at[h]) for h in range(heads)]
+        for copy in sums:
+            copy.start()
 
     def project(x, start, count):
         kv = jnp.dot(x, w_ref[...], preferred_element_type=F32)
-        kv = (kv + b_ref[...]) * rstd_ref[pl.ds(start, count), :]
+        rows = [rstd_ref[i : i + 1, :] for i in range(start // 128, (start + count) // 128)]
+        scale = jnp.concatenate([jnp.broadcast_to(row, (128, 128)).T for row in rows], axis=0)
+        kv = kv + b_ref[...]
         lane = lax.broadcasted_iota(jnp.int32, (count, 2 * size), 1)
         for h in range(heads):
-            mine = kv[:, 2 * size * h : 2 * size * (h + 1)].astype(BF16)
+            mine = (kv[:, 2 * size * h : 2 * size * (h + 1)] * scale).astype(BF16)
             k_ref[h, pl.ds(start, count), :] = jnp.where(lane < size, mine, jnp.ones_like(mine))
             v_ref[h, :size, pl.ds(start, count)] = mine.T[size:, :]
 
@@ -88,12 +93,14 @@
 
     for h in range(heads):
         acc_ref, m_ref = acc_refs[h], m_refs[h]
+        if not first:
+            sums[h].wait()
         for t in range(0, tokens, BLOCK):
             more = add(h, pl.ds(t, min(BLOCK, tokens - t)))
             if t > 0:
                 acc_ref[...] += more
             else:
-                acc_ref[...] = more if first else acc_ins[h][...] + more
+                acc_ref[...] = more if first else acc_bufs[h] + more
 
         @pl.when(jnp.logical_not(jnp.max(acc_ref[size : size + 8, :]) < LIMIT))
         def _(h=h, acc_ref=acc_ref, m_ref=m_ref):
@@ -110,7 +117,7 @@
             if first:
                 acc_ref[...] = jnp.zeros((ROWS, latents), F32)
             else:
-                acc_ref[...] = acc_ins[h][...] * jnp.exp2(before - m_ref[...])
+                acc_ref[...] = acc_bufs[h] * jnp.exp2(before - m_ref[...])
 
             def redo(t, carry):
                 acc_ref[...] += add(h, at(t))
@@ -154,7 +161,7 @@
     heads, size, latents = q.shape
     first = at is None
     vmem = pl.BlockSpec(memory_space=pltpu.VMEM)
-    tokens = rstd.shape[0]
+    tokens = rstd.size
     accs = [jax.ShapeDtypeStruct((ROWS, latents), F32)] * heads
     ms = [jax.ShapeDtypeStruct((1, latents), F32)] * heads
     scratch = [
@@ -168,12 +175,14 @@
         count = x.shape[0] - tokens
         ins = (at, x, rstd, w, b, q, *state)
         in_specs = [pl.BlockSpec(memory_space=pltpu.SMEM), pl.BlockSpec(memory_space=pl.ANY)]
-        in_specs += [vmem] * (len(ins) - 2)
+        in_specs += [vmem] * 4 + [pl.BlockSpec(memory_space=pl.ANY)] * heads + [vmem] * heads
         out = [jax.ShapeDtypeStruct((latents // 64, PAY, 128), BF16)] * heads
         scratch = [pltpu.VMEM(i.shape, F32) for i in accs + ms] + scratch
         scratch += [
             pltpu.VMEM((tokens // count, count, x.shape[1]), BF16),
             pltpu.SemaphoreType.DMA((tokens // count,)),
+            pltpu.VMEM((heads, ROWS, latents), F32),
+            pltpu.SemaphoreType.DMA((heads,)),
         ]
     work = tokens * latents * heads
     return pl.pallas_call(
@@ -279,7 +288,7 @@
     mean = jnp.mean(embed, axis=-1, keepdims=True)
     var = jnp.mean((embed - mean) * (embed - mean), axis=-1)
     rstd = lax.rsqrt(var + 1e-05)
-    mine = rstd.reshape(-1, 1)
+    mine = rstd.reshape(-1, 128)
     rstd = exchange(jnp.broadcast_to(rstd[None], (lax.axis_size("z"), tokens)), "z")
     at = lax.axis_index("z")
     turned = lax.dynamic_slice_in_dim(jnp.concatenate([rstd, rstd]), at + 1, rstd.shape[0] - 1, axis=0)
@@ -294,7 +303,7 @@
 
     weights = (jnp.concatenate([fold[0], fold[1]], axis=1), fold_bias.reshape(1, -1), q_pair)
     state = attend(patches, mine, *weights)
-    other, own = attend(gathered, turned.reshape(-1, 1), *weights, at.reshape(1), state)
+    other, own = attend(gathered, turned.reshape(-1, 128), *weights, at.reshape(1), state)
 
     with jax.named_scope("totals"):
         part = exchange(combine(own, shift(other, "c", 1)), ("y", "x"))

time: 185 us -> 185 us (level)
  starting transfers between devices: 16.6 us -> 33.1 us
  Pallas kernels: 63.5 us -> 49.1 us
    ppermute x3, starting transfers between devices: 6.28 us -> 22.8 us  [shift(): lax.ppermute(block, axis, [(i, (i + by) % size) for i in range(size)])]
    pallas_call x2, Pallas kernels: 57.9 us -> 43.4 us  [attend(): pl.pallas_call(functools.partial(attend_kernel, first), out_shape=out, in...]
  transfers between devices with their start and end apart: 5 -> 5, of which waited for: 3 -> 3; matrix products, arithmetic and copies ran while one was open for 7% -> 6% of each run, Pallas kernels for 4% -> 5%
where the time goes in v6:
time: 185 us; the launch traced here: 184 us
  Pallas kernels  49.1 us (27%)
  blocking collectives  40.5 us (22%)
  waiting for transfers between devices  35.6 us (19%)
  starting transfers between devices  33.1 us (18%)
  between operations  14.2 us (8%)
  matrix products  4.68 us (3%)
  other arithmetic  4.11 us (2%)
  local copies, waits for them, and re-layouts  3.06 us (2%)
    pallas_call x2, Pallas kernels, attend(): pl.pallas_call(functools.partial(attend_kernel, first), out_shape=out, in...  43.4 us
    all_to_all x2, blocking collectives, exchange(): return lax.all_to_all(parts, axis, split_axis=0, concat_axis=0, tiled=True)  40.5 us
    all_gather x1, waiting for transfers between devices, body(): gathered = lax.all_gather(patches, 'z', axis=0, tiled=True)  27.2 us
    ppermute x3, starting transfers between devices, shift(): lax.ppermute(block, axis, [(i, (i + by) % size) for i in range(size)])  22.8 us
    all_to_all x1, starting transfers between devices, exchange(): return lax.all_to_all(parts, axis, split_axis=0, concat_axis=0, tiled=True)  10.3 us
    all_to_all x1, waiting for transfers between devices, exchange(): return lax.all_to_all(parts, axis, split_axis=0, concat_axis=0, tiled=True)  6.26 us
  transfers between devices with their start and end apart: 5, of which 3 were waited for; matrix products, arithmetic and copies ran while one was open for 6% of the time, Pallas kernels for 5%

profile of v6, /device:TPU:8, one launch (start us, length us, event | category | flops | bytes accessed | tf_op | source)
XLA Modules:
  0.0 184.3 jit_solution(14863482869268917536)
XLA Ops:
  6.5 0.0 all-gather.2.cloned.1.call-start
  6.5 0.7 all-gather.2.cloned.1.call-update
  7.3 1.1 copy.9
  8.3 1.9 %collective-permute-start = (bf16[1024,128]{0,1:T(8,128)(2,1)S(1)}, bf16[1024,128]{0,1:T(8,128)(2,1)S(1)}, u32[]{:S(2)}, u32[]{:S(2)}) collective-permute-start(bf16[1024,128]{0,1:T(8,128)(2,1)S(1)} %copy.9), channel_id=1, source_target_pairs={{0,1},{1,0},{2,3},{3,2},{4,5},{5,4},{6,7},{7,6},{8,9},{9,8},{10,11... | collective-permute-start | bytes 786440 | tf_op jit(solution)/shard_map/ppermute | solution.py:276
  10.3 2.4 %collective-permute-start.1 = (bf16[64,2048]{1,0:T(8,128)(2,1)}, bf16[64,2048]{1,0:T(8,128)(2,1)S(1)}, u32[]{:S(2)}, u32[]{:S(2)}) collective-permute-start(bf16[64,2048]{1,0:T(8,128)(2,1)} %bitcast.41), channel_id=1, source_target_pairs={{0,1},{1,0},{2,3},{3,2},{4,5},{5,4},{6,7},{7,6},{8,9},{9,8},{10,11... | collective-permute-start | bytes 786440 | tf_op jit(solution)/shard_map/ppermute | solution.py:276
  12.7 2.4 %fusion.15 = (f32[384]{0:T(512)S(1)}, f32[384,1024]{1,0:T(8,128)S(1)}) fusion(f32[1024]{0:T(1024)} %param.7, bf16[384,768]{1,0:T(8,128)(2,1)} %refs_0_.1, bf16[768,1024]{1,0:T(8,128)(2,1)} %param.6), kind=kOutput, calls=%fused_computation.26 | convolution fusion | flops 604765824 | bytes 3741184 | tf_op jit(solution)/shard_map/dot_general | solution.py:287
  15.1 0.0 copy-start.3
  15.1 0.0 copy-start
  15.1 0.3 multiply_reduce_fusion
  15.4 0.6 fusion.14
  16.0 0.6 broadcast_in_dim.8
  16.6 10.3 %all-to-all-start = ((f32[8,1,384]{2,1,0:T(1,128)}), f32[8,1,384]{2,1,0:T(1,128)S(1)}, u32[]{:S(2)}, u32[]{:S(2)}) async-start(f32[8,1,384]{2,1,0:T(1,128)} %broadcast_in_dim.8), calls=%async_computation | async-start | bytes 24576 | tf_op jit(solution)/shard_map/all_to_all | solution.py:271
  26.9 0.0 copy-done.3
  27.0 0.6 reduce_sum.39
  28.2 0.0 copy-done
  28.2 0.3 convert_reduce_fusion
  28.5 6.3 %all-to-all-done = f32[8,1,384]{2,1,0:T(1,128)S(1)} async-done(((f32[8,1,384]{2,1,0:T(1,128)}), f32[8,1,384]{2,1,0:T(1,128)S(1)}, u32[]{:S(2)}, u32[]{:S(2)}) %all-to-all-start) | async-done | bytes 12320 | tf_op jit(solution)/shard_map/all_to_all | solution.py:271
  34.8 0.6 reshape.47.refs_2_
  35.4 0.0 collective-permute-done
  35.4 0.1 pad_maximum_fusion
  35.5 0.5 fusion.16
  36.0 1.8 fusion.10
  37.8 0.0 copy-start.2
  37.8 0.8 pad_maximum_fusion.2.refs_2_.refs_3_
  38.6 0.6 broadcast_multiply_fusion.2
  39.2 0.0 collective-permute-done.1
  39.2 0.0 copy-done.2
  39.2 0.9 pad_maximum_fusion.1.refs_4_.refs_5_
  40.1 10.1 %attend.2 = (f32[80,2048]{1,0:T(8,128)}, f32[80,2048]{1,0:T(8,128)}, f32[1,2048]{1,0:T(1,128)}, f32[1,2048]{1,0:T(1,128)}) custom-call(bf16[384,768]{1,0:T(8,128)(2,1)} %refs_0_.1, f32[3,128]{1,0:T(4,128)} %get-tuple-element.19.refs_1_, bf16[768,256]{1,0:T(8,128)(2,1)} %pad_maximum_fusion.2.refs_2_.refs_3_, f32[1,256]{1,0:T(1,128)} %bitcast.49, ...), custom_call_target="tpu_custom_call" | custom-call | flops 1610612736 | bytes 589824 | tf_op jit(solution)/shard_map/attend/pallas_call | solution.py:188
  50.2 27.2 %all-gather.2.cloned.1.call-done.refs_1_ = bf16[3072,768]{1,0:T(8,128)(2,1)} async-done(((bf16[384,768]{1,0:T(8,128)(2,1)}), bf16[3072,768]{1,0:T(8,128)(2,1)}) %all-gather.2.cloned.1.call-update) | async-done | bytes 4718608 | tf_op jit(solution)/shard_map/all_gather | solution.py:282
  77.3 33.3 %attend.3 = (bf16[32,40,128]{2,1,0:T(8,128)(2,1)}, bf16[32,40,128]{2,1,0:T(8,128)(2,1)}) custom-call(s32[1]{0:T(128)} %bitcast.refs_0_, bf16[3072,768]{1,0:T(8,128)(2,1)} %all-gather.2.cloned.1.call-done.refs_1_, f32[21,128]{1,0:T(8,128)} %reshape.47.refs_2_, bf16[768,256]{1,0:T(8,128)(2,1)} %pad_maximum_fusion.2.refs_2_.refs_3_, f32[1,256]{1,0:T(1,128)} %bitcast.50, ...), custom_call_target="tpu_custom_call" | custom-call | flops 11274289152 | bytes 4128768 | tf_op jit(solution)/shard_map/attend/pallas_call | solution.py:188
  110.7 18.4 %collective-permute-start.2 = (bf16[32,40,128]{2,1,0:T(8,128)(2,1)}, bf16[32,40,128]{2,1,0:T(8,128)(2,1)S(1)}, u32[]{:S(2)}, u32[]{:S(2)}) collective-permute-start(bf16[32,40,128]{2,1,0:T(8,128)(2,1)} %get-tuple-element.16), channel_id=1, source_target_pairs={{0,1},{1,0},{2,3},{3,2},{4,5},{5,4},{6,7},{7,6},{8,9},{9,8},{10,11... | collective-permute-start | bytes 983048 | tf_op jit(solution)/shard_map/totals/ppermute | solution.py:276
  129.1 1.4 collective-permute-done.2.two_ref
  130.5 0.0 copy-start.1
  130.5 0.7 copy-done.1
  131.3 2.0 %combine.1 = bf16[32,40,128]{2,1,0:T(8,128)(2,1)} custom-call(bf16[32,40,128]{2,1,0:T(8,128)(2,1)} %get-tuple-element.15.one_ref, bf16[32,40,128]{2,1,0:T(8,128)(2,1)} %copy-done.1), custom_call_target="tpu_custom_call" | custom-call | tf_op jit(solution)/shard_map/totals/combine/pallas_call | solution.py:228
  133.3 24.2 %all_to_all.19.parts_ref = bf16[32,40,128]{2,1,0:T(8,128)(2,1)} all-to-all(bf16[32,40,128]{2,1,0:T(8,128)(2,1)} %combine.1), channel_id=1, replica_groups=mesh['y'=8,'x'=4,'z'=8,'c'=2] {'y','x'}, dimensions={0} | all-to-all | bytes 655360 | tf_op jit(solution)/shard_map/totals/all_to_all | solution.py:271
  157.5 1.8 finish.1
  159.3 16.3 %all_to_all.20.parts_ref = bf16[32,32,128]{2,1,0:T(8,128)(2,1)} all-to-all(bf16[32,32,128]{2,1,0:T(8,128)(2,1)} %finish.1), channel_id=1, replica_groups=mesh['y'=8,'x'=4,'z'=8,'c'=2] {'y','x'}, dimensions={0} | all-to-all | bytes 524288 | tf_op jit(solution)/shard_map/readout/all_to_all | solution.py:271
  175.6 1.8 place.1
  (7 shorter events, 0.1 us)
Async XLA Ops:
  6.5 70.8 %all-gather.2.cloned.1.call-start = ((), (), s32[]{:S(2)}) async-start(), calls=%async_computation.3 | async-start | bytes 5308416 | tf_op jit(solution)/shard_map/all_gather | solution.py:282
  8.3 27.1 %collective-permute-start = (bf16[1024,128]{0,1:T(8,128)(2,1)S(1)}, bf16[1024,128]{0,1:T(8,128)(2,1)S(1)}, u32[]{:S(2)}, u32[]{:S(2)}) collective-permute-start(bf16[1024,128]{0,1:T(8,128)(2,1)S(1)} %copy.9), channel_id=1, source_target_pairs={{0,1},{1,0},{2,3},{3,2},{4,5},{5,4},{6,7},{7,6},{8,9},{9,8},{10,11... | collective-permute-start | bytes 786440 | tf_op jit(solution)/shard_map/ppermute | solution.py:276
  10.3 28.9 %collective-permute-start.1 = (bf16[64,2048]{1,0:T(8,128)(2,1)}, bf16[64,2048]{1,0:T(8,128)(2,1)S(1)}, u32[]{:S(2)}, u32[]{:S(2)}) collective-permute-start(bf16[64,2048]{1,0:T(8,128)(2,1)} %bitcast.41), channel_id=1, source_target_pairs={{0,1},{1,0},{2,3},{3,2},{4,5},{5,4},{6,7},{7,6},{8,9},{9,8},{10,11... | collective-permute-start | bytes 786440 | tf_op jit(solution)/shard_map/ppermute | solution.py:276
  15.1 11.9 %copy-start.3 = (f32[1024]{0:T(1024)S(1)}, f32[1024]{0:T(1024)}, u32[]{:S(2)}) copy-start(f32[1024]{0:T(1024)} %param.7) | copy-start | bytes 12292
  15.1 13.1 %copy-start = (bf16[768,1024]{1,0:T(8,128)(2,1)S(1)}, bf16[768,1024]{1,0:T(8,128)(2,1)}, u32[]{:S(2)}) copy-start(bf16[768,1024]{1,0:T(8,128)(2,1)} %param.6) | copy-start | bytes 4718596
  16.6 18.2 %all-to-all-start = ((f32[8,1,384]{2,1,0:T(1,128)}), f32[8,1,384]{2,1,0:T(1,128)S(1)}, u32[]{:S(2)}, u32[]{:S(2)}) async-start(f32[8,1,384]{2,1,0:T(1,128)} %broadcast_in_dim.8), calls=%async_computation | async-start | bytes 24576 | tf_op jit(solution)/shard_map/all_to_all | solution.py:271
  37.8 1.4 copy-start.2
  110.7 19.9 %collective-permute-start.2 = (bf16[32,40,128]{2,1,0:T(8,128)(2,1)}, bf16[32,40,128]{2,1,0:T(8,128)(2,1)S(1)}, u32[]{:S(2)}, u32[]{:S(2)}) collective-permute-start(bf16[32,40,128]{2,1,0:T(8,128)(2,1)} %get-tuple-element.16), channel_id=1, source_target_pairs={{0,1},{1,0},{2,3},{3,2},{4,5},{5,4},{6,7},{7,6},{8,9},{9,8},{10,11... | collective-permute-start | bytes 983048 | tf_op jit(solution)/shard_map/totals/ppermute | solution.py:276
  130.5 0.7 copy-start.1
Sparse Core Ops, SparseCore 0:
  9.4 67.8 all-gather.1
